TPU v7x, 256 devices: a whole 4x4x8 slice. The times are simulated.
256 devices in a mesh: segment: 4 (over y), blk: 64 (over x, z, core).
Axes of the slice: x: 4, y: 4, z: 8, core: 2. Of those that a mesh axis runs over, the one named last changes fastest.
Arguments:
- inputs: bfloat16 [4, 1024, 64, 128], P(None, 'blk'), may hold values from -6 to 6
- weights: bfloat16 [8, 1024, 64, 2048], P('segment', 'blk'), may hold values from -0.1875 to 0.1875
- biases: float32 [8, 1024, 64], P('segment', 'blk'), may hold values from -3 to 3
- tile_index: int32 [8, 1024, 32], P('segment', 'blk'), may hold values from 0 to 31, each once within a row
Outputs:
- final_activity: bfloat16 [4, 1024, 64, 128], P('segment', 'blk')
Inputs may be any that keep to these rules, and one draw needn't show every extreme that they name: `tile_index`: each row of 32 entries names every member 0..31 once.
All inputs are finite; a program needn't handle non-finite values.
Results may differ from a plain program's by a relative error of at most 0.014.
Values may be sent and summed in bfloat16 or wider, within the bound.
A program may use at most 128 MiB of HBM per device.

v0:
```python
import jax
import jax.numpy as jnp
from jax import lax
from jax.sharding import PartitionSpec as P


def from_partner(array, axis, stride):
    return lax.ppermute(array, axis, [(i, i ^ 1 << stride) for i in range(lax.axis_size(axis))])


def passed_along(value, axis, steps):
    count = lax.axis_size(axis)
    initial, last = (max(0, -steps), min(count, count - steps))
    return lax.ppermute(value, axis, [(source, source + steps) for source in range(initial, last)])


def permuted_weights(weights, tile_index):
    blocks, tile_size, row_width = weights.shape
    fan_count = tile_index.shape[1]
    shaped = weights.reshape(blocks, tile_size, fan_count, row_width // fan_count)
    onehot = (
        tile_index[:, :, None] == jnp.arange(fan_count, dtype=jnp.int32)[None, None, :]
    ).astype(jnp.bfloat16)
    placed = jnp.einsum("jakc,jkm->jamc", shaped, onehot, preferred_element_type=jnp.float32)
    return placed.astype(jnp.bfloat16).reshape(blocks * tile_size, row_width)


def join_group(activity, bit_place):
    partner = from_partner(activity, "blk", bit_place)
    upper_half = lax.axis_index("blk") // (1 << bit_place) % 2
    first_order = jnp.concatenate([activity, partner], axis=0)
    second = jnp.concatenate([partner, activity], axis=0)
    return jnp.where(upper_half == 0, first_order, second)


def apply_layer(activity, bit_place, matrix, offset):
    grouped = join_group(activity, bit_place)
    members, tile_size, batch_size = grouped.shape
    flat_group = grouped.reshape(members * tile_size, batch_size)
    summed = jnp.dot(matrix, flat_group, preferred_element_type=jnp.float32)
    summed = summed.reshape(activity.shape) + offset[:, :, None]
    return jnp.maximum(summed, 0.0).astype(jnp.bfloat16)


def regroup_segmented(activity, group_size):
    local_blocks, tile_size, batch_size = activity.shape
    position = lax.axis_index("blk")
    for level_index in range(group_size.bit_length() - 1):
        shaped = activity.reshape(
            local_blocks >> level_index + 1, 2, 1 << level_index, tile_size, batch_size
        )
        own_bit = (position >> level_index + 1) % 2
        outgoing = lax.dynamic_index_in_dim(shaped, 1 - own_bit, 1, keepdims=True)
        incoming = from_partner(outgoing, "blk", level_index + 1)
        shaped = lax.dynamic_update_index_in_dim(shaped, incoming, 1 - own_bit, 1)
        activity = shaped.reshape(local_blocks, tile_size, batch_size)
    return activity


def body(inputs, weights, biases, tile_index):
    segments = lax.axis_size("segment")
    segment_index = lax.axis_index("segment")
    devices = lax.axis_size("blk")
    local_blocks = inputs.shape[1]
    group_size = min(local_blocks, devices // 4)
    far_bit = (2 * group_size).bit_length() - 1
    micro_count = inputs.shape[0]
    matrices = [
        permuted_weights(weights[layer_index], tile_index[layer_index]) for layer_index in range(2)
    ]
    results = jnp.zeros(inputs.shape, jnp.bfloat16)
    arriving = jnp.zeros(inputs.shape[1:], jnp.bfloat16)
    step_count = micro_count + segments - 1
    for step_index in range(step_count):
        new_input = inputs[min(step_index, micro_count - 1)]
        present = jnp.where(segment_index == 0, new_input, arriving)
        present = apply_layer(present, 0, matrices[0], biases[0])
        present = regroup_segmented(present, group_size)
        present = apply_layer(present, far_bit, matrices[1], biases[1])
        present = regroup_segmented(present, group_size)
        finished = step_index - (segments - 1)
        if finished >= 0:
            results = results.at[finished].set(present)
        if step_index + 1 < step_count:
            arriving = passed_along(present, "segment", 1)
    gathered = lax.all_to_all(results[:, None], "segment", split_axis=0, concat_axis=1, tiled=True)
    return gathered[:, segments - 1]


def solution(mesh):
    in_specs = (
        P(None, "blk", None, None),
        P("segment", "blk", None, None),
        P("segment", "blk", None),
        P("segment", "blk", None),
    )
    out_specs = P("segment", "blk", None, None)
    return jax.shard_map(body, mesh=mesh, in_specs=in_specs, out_specs=out_specs, check_vma=False)
```

profile of v0, /device:TPU:96, one launch (start us, length us, event | category | flops | bytes accessed | tf_op | source)
XLA Modules:
  0.0 690.5 jit_solution(18264248735898804815)
XLA Ops:
  1.1 6.3 fusion.328
  7.4 12.9 %reshape_squeeze.7 = bf16[16,64,32,64]{3,2,1,0:T(8,128)(2,1)} reshape(bf16[1,16,64,2048]{3,2,1,0:T(8,128)(2,1)} %get-tuple-element.53) | data formatting | bytes 8388608 | tf_op jit(solution)/shard_map/reshape;squeeze | solution.py:20
  20.3 9.1 %convert_bitcast_fusion = bf16[16,64,32,64]{3,2,1,0:T(8,128)(2,1)} fusion(bf16[16,64,32,64]{3,2,1,0:T(8,128)(2,1)} %reshape_squeeze.7, s32[16,32]{1,0:T(8,128)S(1)} %get-tuple-element.57), kind=kOutput, calls=%fused_computation | convolution fusion | flops 136331264 | bytes 8390656 | tf_op jit(solution)/shard_map/jakc,jkm->jamc/dot_general | solution.py:24
  29.3 9.2 %fusion.163 = bf16[16,64,128]{2,1,0:T(8,128)(2,1)S(1)} fusion(bf16[16,64,32,64]{3,2,1,0:T(8,128)(2,1)} %convert_bitcast_fusion, bf16[16,64,128]{2,1,0:T(8,128)(2,1)S(1)} %collective-permute-done, bf16[16,64,128]{2,1,0:T(8,128)(2,1)S(1)} %select_bitcast_fusion, pred[]{:T(512)S(6)} %eq.137, f32[16,64]{1,0:T(8,128)S(1)} %get-tuple-element.56), kind=kOutput, calls=%fused_computation.75 | convolution fusion | flops 538050560 | bytes 4984833 | tf_op jit(solution)/shard_map/dot_general | solution.py:40
  38.8 5.8 collective-permute-done.1
  44.7 8.6 %collective-permute-done.2 = bf16[4,1,2,64,128]{4,3,2,1,0:T(8,128)(2,1)S(1)} collective-permute-done((bf16[4,1,2,64,128]{4,3,2,1,0:T(8,128)(2,1)S(1)}, bf16[4,1,2,64,128]{4,3,2,1,0:T(8,128)(2,1)S(1)}, u32[]{:S(2)}, u32[]{:S(2)}) %collective-permute-start.2) | collective-permute-done | bytes 131104 | tf_op jit(solution)/shard_map/ppermute | solution.py:8
  58.2 7.5 %collective-permute-done.3 = bf16[2,1,4,64,128]{4,3,2,1,0:T(8,128)(2,1)S(1)} collective-permute-done((bf16[2,1,4,64,128]{4,3,2,1,0:T(8,128)(2,1)S(1)}, bf16[2,1,4,64,128]{4,3,2,1,0:T(8,128)(2,1)S(1)}, u32[]{:S(2)}, u32[]{:S(2)}) %collective-permute-start.3) | collective-permute-done | bytes 131104 | tf_op jit(solution)/shard_map/ppermute | solution.py:8
  67.4 12.9 %reshape_squeeze.6 = bf16[16,64,32,64]{3,2,1,0:T(8,128)(2,1)} reshape(bf16[1,16,64,2048]{3,2,1,0:T(8,128)(2,1)} %get-tuple-element.54) | data formatting | bytes 8388608 | tf_op jit(solution)/shard_map/reshape;squeeze | solution.py:20
  83.1 9.0 %convert_bitcast_fusion.1 = bf16[16,64,32,64]{3,2,1,0:T(8,128)(2,1)} fusion(bf16[16,64,32,64]{3,2,1,0:T(8,128)(2,1)} %reshape_squeeze.6, s32[16,32]{1,0:T(8,128)S(1)} %get-tuple-element.58), kind=kOutput, calls=%fused_computation.1 | convolution fusion | flops 136331264 | bytes 8390656 | tf_op jit(solution)/shard_map/jakc,jkm->jamc/dot_general | solution.py:24
  92.1 9.2 %fusion.184 = bf16[16,64,128]{2,1,0:T(8,128)(2,1)S(1)} fusion(bf16[16,64,32,64]{3,2,1,0:T(8,128)(2,1)} %convert_bitcast_fusion.1, bf16[16,64,128]{2,1,0:T(8,128)(2,1)S(1)} %collective-permute-done.5, bf16[16,64,128]{2,1,0:T(8,128)(2,1)S(1)} %bitcast.344, pred[]{:T(512)S(6)} %eq.132, f32[16,64]{1,0:T(8,128)S(1)} %get-tuple-element.55), kind=kOutput, calls=%fused_computation.82 | convolution fusion | flops 538050560 | bytes 4984833 | tf_op jit(solution)/shard_map/dot_general | solution.py:40
  101.5 5.0 collective-permute-done.6
  106.8 6.7 collective-permute-done.7
  116.8 6.5 collective-permute-done.8
  137.5 10.0 %fusion.160 = bf16[16,64,128]{2,1,0:T(8,128)(2,1)S(1)} fusion(bf16[16,64,32,64]{3,2,1,0:T(8,128)(2,1)} %convert_bitcast_fusion, bf16[16,64,128]{2,1,0:T(8,128)(2,1)S(1)} %collective-permute-done.11, bf16[16,64,128]{2,1,0:T(8,128)(2,1)S(1)} %bitcast_select_fusion, pred[]{:T(512)S(6)} %eq.137, f32[16,64]{1,0:T(8,128)S(1)} %get-tuple-element.56), kind=kOutput, calls=%fused_computation.74 | convolution fusion | flops 538050560 | bytes 4984833 | tf_op jit(solution)/shard_map/dot_general | solution.py:40
  152.9 7.2 %collective-permute-done.13 = bf16[4,1,2,64,128]{4,3,2,1,0:T(8,128)(2,1)S(1)} collective-permute-done((bf16[4,1,2,64,128]{4,3,2,1,0:T(8,128)(2,1)S(1)}, bf16[4,1,2,64,128]{4,3,2,1,0:T(8,128)(2,1)S(1)}, u32[]{:S(2)}, u32[]{:S(2)}) %collective-permute-start.13) | collective-permute-done | bytes 131104 | tf_op jit(solution)/shard_map/ppermute | solution.py:8
  163.5 7.9 %collective-permute-done.14 = bf16[2,1,4,64,128]{4,3,2,1,0:T(8,128)(2,1)S(1)} collective-permute-done((bf16[2,1,4,64,128]{4,3,2,1,0:T(8,128)(2,1)S(1)}, bf16[2,1,4,64,128]{4,3,2,1,0:T(8,128)(2,1)S(1)}, u32[]{:S(2)}, u32[]{:S(2)}) %collective-permute-start.14) | collective-permute-done | bytes 131104 | tf_op jit(solution)/shard_map/ppermute | solution.py:8
  177.9 7.8 %collective-permute-done.16 = bf16[16,64,128]{2,1,0:T(8,128)(2,1)S(1)} collective-permute-done((bf16[16,64,128]{2,1,0:T(8,128)(2,1)S(1)}, bf16[16,64,128]{2,1,0:T(8,128)(2,1)S(1)}, u32[]{:S(2)}, u32[]{:S(2)}) %collective-permute-start.16) | collective-permute-done | bytes 262176 | tf_op jit(solution)/shard_map/ppermute | solution.py:8
  185.7 6.2 fusion.181
  197.1 7.0 %collective-permute-done.18 = bf16[4,1,2,64,128]{4,3,2,1,0:T(8,128)(2,1)S(1)} collective-permute-done((bf16[4,1,2,64,128]{4,3,2,1,0:T(8,128)(2,1)S(1)}, bf16[4,1,2,64,128]{4,3,2,1,0:T(8,128)(2,1)S(1)}, u32[]{:S(2)}, u32[]{:S(2)}) %collective-permute-start.18) | collective-permute-done | bytes 131104 | tf_op jit(solution)/shard_map/ppermute | solution.py:8
  208.5 5.9 collective-permute-done.19
  214.6 5.0 collective-permute-done.20
  229.7 6.2 fusion.157
  235.9 5.5 collective-permute-done.23
  241.6 8.4 %collective-permute-done.24 = bf16[4,1,2,64,128]{4,3,2,1,0:T(8,128)(2,1)S(1)} collective-permute-done((bf16[4,1,2,64,128]{4,3,2,1,0:T(8,128)(2,1)S(1)}, bf16[4,1,2,64,128]{4,3,2,1,0:T(8,128)(2,1)S(1)}, u32[]{:S(2)}, u32[]{:S(2)}) %collective-permute-start.24) | collective-permute-done | bytes 131104 | tf_op jit(solution)/shard_map/ppermute | solution.py:8
  253.1 8.8 %collective-permute-done.25 = bf16[2,1,4,64,128]{4,3,2,1,0:T(8,128)(2,1)S(1)} collective-permute-done((bf16[2,1,4,64,128]{4,3,2,1,0:T(8,128)(2,1)S(1)}, bf16[2,1,4,64,128]{4,3,2,1,0:T(8,128)(2,1)S(1)}, u32[]{:S(2)}, u32[]{:S(2)}) %collective-permute-start.25) | collective-permute-done | bytes 131104 | tf_op jit(solution)/shard_map/ppermute | solution.py:8
  262.0 5.4 collective-permute-done.26
  268.5 8.1 %collective-permute-done.27 = bf16[16,64,128]{2,1,0:T(8,128)(2,1)S(1)} collective-permute-done((bf16[16,64,128]{2,1,0:T(8,128)(2,1)S(1)}, bf16[16,64,128]{2,1,0:T(8,128)(2,1)S(1)}, u32[]{:S(2)}, u32[]{:S(2)}) %collective-permute-start.27) | collective-permute-done | bytes 262176 | tf_op jit(solution)/shard_map/ppermute | solution.py:8
  276.6 6.2 fusion.178
  282.9 5.0 collective-permute-done.28
  288.0 6.8 collective-permute-done.29
  297.9 7.3 %collective-permute-done.30 = bf16[2,1,4,64,128]{4,3,2,1,0:T(8,128)(2,1)S(1)} collective-permute-done((bf16[2,1,4,64,128]{4,3,2,1,0:T(8,128)(2,1)S(1)}, bf16[2,1,4,64,128]{4,3,2,1,0:T(8,128)(2,1)S(1)}, u32[]{:S(2)}, u32[]{:S(2)}) %collective-permute-start.30) | collective-permute-done | bytes 131104 | tf_op jit(solution)/shard_map/ppermute | solution.py:8
  320.6 6.2 fusion.154
  326.8 5.5 collective-permute-done.34
  332.5 8.4 %collective-permute-done.35 = bf16[4,1,2,64,128]{4,3,2,1,0:T(8,128)(2,1)S(1)} collective-permute-done((bf16[4,1,2,64,128]{4,3,2,1,0:T(8,128)(2,1)S(1)}, bf16[4,1,2,64,128]{4,3,2,1,0:T(8,128)(2,1)S(1)}, u32[]{:S(2)}, u32[]{:S(2)}) %collective-permute-start.35) | collective-permute-done | bytes 131104 | tf_op jit(solution)/shard_map/ppermute | solution.py:8
  344.0 8.8 %collective-permute-done.36 = bf16[2,1,4,64,128]{4,3,2,1,0:T(8,128)(2,1)S(1)} collective-permute-done((bf16[2,1,4,64,128]{4,3,2,1,0:T(8,128)(2,1)S(1)}, bf16[2,1,4,64,128]{4,3,2,1,0:T(8,128)(2,1)S(1)}, u32[]{:S(2)}, u32[]{:S(2)}) %collective-permute-start.36) | collective-permute-done | bytes 131104 | tf_op jit(solution)/shard_map/ppermute | solution.py:8
  359.4 8.1 %collective-permute-done.38 = bf16[16,64,128]{2,1,0:T(8,128)(2,1)S(1)} collective-permute-done((bf16[16,64,128]{2,1,0:T(8,128)(2,1)S(1)}, bf16[16,64,128]{2,1,0:T(8,128)(2,1)S(1)}, u32[]{:S(2)}, u32[]{:S(2)}) %collective-permute-start.38) | collective-permute-done | bytes 262176 | tf_op jit(solution)/shard_map/ppermute | solution.py:8
  367.5 6.2 fusion.175
  378.9 6.8 collective-permute-done.40
  388.7 7.3 %collective-permute-done.41 = bf16[2,1,4,64,128]{4,3,2,1,0:T(8,128)(2,1)S(1)} collective-permute-done((bf16[2,1,4,64,128]{4,3,2,1,0:T(8,128)(2,1)S(1)}, bf16[2,1,4,64,128]{4,3,2,1,0:T(8,128)(2,1)S(1)}, u32[]{:S(2)}, u32[]{:S(2)}) %collective-permute-start.41) | collective-permute-done | bytes 131104 | tf_op jit(solution)/shard_map/ppermute | solution.py:8
  411.3 6.2 fusion.166
  417.5 5.5 collective-permute-done.45
  423.2 8.4 %collective-permute-done.46 = bf16[4,1,2,64,128]{4,3,2,1,0:T(8,128)(2,1)S(1)} collective-permute-done((bf16[4,1,2,64,128]{4,3,2,1,0:T(8,128)(2,1)S(1)}, bf16[4,1,2,64,128]{4,3,2,1,0:T(8,128)(2,1)S(1)}, u32[]{:S(2)}, u32[]{:S(2)}) %collective-permute-start.46) | collective-permute-done | bytes 131104 | tf_op jit(solution)/shard_map/ppermute | solution.py:8
  434.7 8.8 %collective-permute-done.47 = bf16[2,1,4,64,128]{4,3,2,1,0:T(8,128)(2,1)S(1)} collective-permute-done((bf16[2,1,4,64,128]{4,3,2,1,0:T(8,128)(2,1)S(1)}, bf16[2,1,4,64,128]{4,3,2,1,0:T(8,128)(2,1)S(1)}, u32[]{:S(2)}, u32[]{:S(2)}) %collective-permute-start.47) | collective-permute-done | bytes 131104 | tf_op jit(solution)/shard_map/ppermute | solution.py:8
  450.3 8.1 %collective-permute-done.49 = bf16[16,64,128]{2,1,0:T(8,128)(2,1)S(1)} collective-permute-done((bf16[16,64,128]{2,1,0:T(8,128)(2,1)S(1)}, bf16[16,64,128]{2,1,0:T(8,128)(2,1)S(1)}, u32[]{:S(2)}, u32[]{:S(2)}) %collective-permute-start.49) | collective-permute-done | bytes 262176 | tf_op jit(solution)/shard_map/ppermute | solution.py:8
  458.4 6.2 fusion.187
  469.8 6.8 collective-permute-done.51
  479.6 7.3 %collective-permute-done.52 = bf16[2,1,4,64,128]{4,3,2,1,0:T(8,128)(2,1)S(1)} collective-permute-done((bf16[2,1,4,64,128]{4,3,2,1,0:T(8,128)(2,1)S(1)}, bf16[2,1,4,64,128]{4,3,2,1,0:T(8,128)(2,1)S(1)}, u32[]{:S(2)}, u32[]{:S(2)}) %collective-permute-start.52) | collective-permute-done | bytes 131104 | tf_op jit(solution)/shard_map/ppermute | solution.py:8
  502.1 6.2 fusion.169
  508.4 5.5 collective-permute-done.56
  514.1 8.4 %collective-permute-done.57 = bf16[4,1,2,64,128]{4,3,2,1,0:T(8,128)(2,1)S(1)} collective-permute-done((bf16[4,1,2,64,128]{4,3,2,1,0:T(8,128)(2,1)S(1)}, bf16[4,1,2,64,128]{4,3,2,1,0:T(8,128)(2,1)S(1)}, u32[]{:S(2)}, u32[]{:S(2)}) %collective-permute-start.57) | collective-permute-done | bytes 131104 | tf_op jit(solution)/shard_map/ppermute | solution.py:8
  525.6 8.8 %collective-permute-done.58 = bf16[2,1,4,64,128]{4,3,2,1,0:T(8,128)(2,1)S(1)} collective-permute-done((bf16[2,1,4,64,128]{4,3,2,1,0:T(8,128)(2,1)S(1)}, bf16[2,1,4,64,128]{4,3,2,1,0:T(8,128)(2,1)S(1)}, u32[]{:S(2)}, u32[]{:S(2)}) %collective-permute-start.58) | collective-permute-done | bytes 131104 | tf_op jit(solution)/shard_map/ppermute | solution.py:8
  541.0 8.1 %collective-permute-done.60 = bf16[16,64,128]{2,1,0:T(8,128)(2,1)S(1)} collective-permute-done((bf16[16,64,128]{2,1,0:T(8,128)(2,1)S(1)}, bf16[16,64,128]{2,1,0:T(8,128)(2,1)S(1)}, u32[]{:S(2)}, u32[]{:S(2)}) %collective-permute-start.60) | collective-permute-done | bytes 262176 | tf_op jit(solution)/shard_map/ppermute | solution.py:8
  549.1 6.2 fusion.190
  560.4 6.8 collective-permute-done.62
  570.3 7.3 %collective-permute-done.63 = bf16[2,1,4,64,128]{4,3,2,1,0:T(8,128)(2,1)S(1)} collective-permute-done((bf16[2,1,4,64,128]{4,3,2,1,0:T(8,128)(2,1)S(1)}, bf16[2,1,4,64,128]{4,3,2,1,0:T(8,128)(2,1)S(1)}, u32[]{:S(2)}, u32[]{:S(2)}) %collective-permute-start.63) | collective-permute-done | bytes 131104 | tf_op jit(solution)/shard_map/ppermute | solution.py:8
  593.1 6.2 fusion.172
  599.3 5.5 collective-permute-done.67
  605.0 8.4 %collective-permute-done.68 = bf16[4,1,2,64,128]{4,3,2,1,0:T(8,128)(2,1)S(1)} collective-permute-done((bf16[4,1,2,64,128]{4,3,2,1,0:T(8,128)(2,1)S(1)}, bf16[4,1,2,64,128]{4,3,2,1,0:T(8,128)(2,1)S(1)}, u32[]{:S(2)}, u32[]{:S(2)}) %collective-permute-start.68) | collective-permute-done | bytes 131104 | tf_op jit(solution)/shard_map/ppermute | solution.py:8
  616.5 8.8 %collective-permute-done.69 = bf16[2,1,4,64,128]{4,3,2,1,0:T(8,128)(2,1)S(1)} collective-permute-done((bf16[2,1,4,64,128]{4,3,2,1,0:T(8,128)(2,1)S(1)}, bf16[2,1,4,64,128]{4,3,2,1,0:T(8,128)(2,1)S(1)}, u32[]{:S(2)}, u32[]{:S(2)}) %collective-permute-start.69) | collective-permute-done | bytes 131104 | tf_op jit(solution)/shard_map/ppermute | solution.py:8
  631.8 8.1 %collective-permute-done.71 = bf16[16,64,128]{2,1,0:T(8,128)(2,1)S(1)} collective-permute-done((bf16[16,64,128]{2,1,0:T(8,128)(2,1)S(1)}, bf16[16,64,128]{2,1,0:T(8,128)(2,1)S(1)}, u32[]{:S(2)}, u32[]{:S(2)}) %collective-permute-start.71) | collective-permute-done | bytes 262176 | tf_op jit(solution)/shard_map/ppermute | solution.py:8
  639.9 6.2 fusion.193
  651.3 6.8 collective-permute-done.73
  661.4 7.1 %collective-permute-done.74 = bf16[2,1,4,64,128]{4,3,2,1,0:T(8,128)(2,1)S(1)} collective-permute-done((bf16[2,1,4,64,128]{4,3,2,1,0:T(8,128)(2,1)S(1)}, bf16[2,1,4,64,128]{4,3,2,1,0:T(8,128)(2,1)S(1)}, u32[]{:S(2)}, u32[]{:S(2)}) %collective-permute-start.74) | collective-permute-done | bytes 131104 | tf_op jit(solution)/shard_map/ppermute | solution.py:8
  673.6 15.9 %all_to_all.12 = bf16[4,1,16,64,128]{4,3,2,1,0:T(8,128)(2,1)S(1)} all-to-all(bf16[4,1,16,64,128]{4,3,2,1,0:T(8,128)(2,1)S(1)} %bitcast_dynamic-update-slice_fusion), channel_id=1, replica_groups=mesh['segment'=4,'blk'=64] {'segment'}, dimensions={0} | all-to-all | bytes 2097152 | tf_op jit(solution)/shard_map/all_to_all | solution.py:86
  (250 shorter events, 212.1 us)
Async XLA Ops:
  1.0 28.4 %collective-permute-start = (bf16[16,64,128]{2,1,0:T(8,128)(2,1)S(1)}, bf16[16,64,128]{2,1,0:T(8,128)(2,1)S(1)}, u32[]{:S(2)}, u32[]{:S(2)}) collective-permute-start(bf16[16,64,128]{2,1,0:T(8,128)(2,1)S(1)} %select_bitcast_fusion), channel_id=1, source_target_pairs={{0,1},{1,0},{2,3},{3,2},{4,5},{5,4},{6,7},{7,6},{8,9},{9,8},{10,11... | collective-permute-start | bytes 786440 | tf_op jit(solution)/shard_map/ppermute | solution.py:8
  38.5 6.0 collective-permute-start.1
  44.6 8.7 %collective-permute-start.2 = (bf16[4,1,2,64,128]{4,3,2,1,0:T(8,128)(2,1)S(1)}, bf16[4,1,2,64,128]{4,3,2,1,0:T(8,128)(2,1)S(1)}, u32[]{:S(2)}, u32[]{:S(2)}) collective-permute-start(bf16[4,1,2,64,128]{4,3,2,1,0:T(8,128)(2,1)S(1)} %constant_dynamic-slice_fusion.54), channel_id=1, source_target_pairs={{0,4},{1,5},{2,6},{3,7},{4,0},{5,1},{6,2},{7,3},{8,12},{9,13},{10,... | collective-permute-start | bytes 393224 | tf_op jit(solution)/shard_map/ppermute | solution.py:8
  53.4 12.4 %collective-permute-start.3 = (bf16[2,1,4,64,128]{4,3,2,1,0:T(8,128)(2,1)S(1)}, bf16[2,1,4,64,128]{4,3,2,1,0:T(8,128)(2,1)S(1)}, u32[]{:S(2)}, u32[]{:S(2)}) collective-permute-start(bf16[2,1,4,64,128]{4,3,2,1,0:T(8,128)(2,1)S(1)} %constant_dynamic-slice_fusion.53), channel_id=1, source_target_pairs={{0,8},{1,9},{2,10},{3,11},{4,12},{5,13},{6,14},{7,15},{8,0},{9,1},... | collective-permute-start | bytes 393224 | tf_op jit(solution)/shard_map/ppermute | solution.py:8
  65.8 14.4 %collective-permute-start.4 = (bf16[1,1,8,64,128]{4,3,2,1,0:T(8,128)(2,1)S(1)}, bf16[1,1,8,64,128]{4,3,2,1,0:T(8,128)(2,1)S(1)}, u32[]{:S(2)}, u32[]{:S(2)}) collective-permute-start(bf16[1,1,8,64,128]{4,3,2,1,0:T(8,128)(2,1)S(1)} %constant_dynamic-slice_fusion.52), channel_id=1, source_target_pairs={{0,16},{1,17},{2,18},{3,19},{4,20},{5,21},{6,22},{7,23},{8,24},{9,... | collective-permute-start | bytes 393224 | tf_op jit(solution)/shard_map/ppermute | solution.py:8
  80.2 11.9 %collective-permute-start.5 = (bf16[16,64,128]{2,1,0:T(8,128)(2,1)S(1)}, bf16[16,64,128]{2,1,0:T(8,128)(2,1)S(1)}, u32[]{:S(2)}, u32[]{:S(2)}) collective-permute-start(bf16[16,64,128]{2,1,0:T(8,128)(2,1)S(1)} %bitcast.343), channel_id=1, source_target_pairs={{0,32},{1,33},{2,34},{3,35},{4,36},{5,37},{6,38},{7,39},{8,40},{9,... | collective-permute-start | bytes 786440 | tf_op jit(solution)/shard_map/ppermute | solution.py:8
  101.4 5.1 collective-permute-start.6
  106.5 7.0 %collective-permute-start.7 = (bf16[4,1,2,64,128]{4,3,2,1,0:T(8,128)(2,1)S(1)}, bf16[4,1,2,64,128]{4,3,2,1,0:T(8,128)(2,1)S(1)}, u32[]{:S(2)}, u32[]{:S(2)}) collective-permute-start(bf16[4,1,2,64,128]{4,3,2,1,0:T(8,128)(2,1)S(1)} %constant_dynamic-slice_fusion.50), channel_id=1, source_target_pairs={{0,4},{1,5},{2,6},{3,7},{4,0},{5,1},{6,2},{7,3},{8,12},{9,13},{10,... | collective-permute-start | bytes 393224 | tf_op jit(solution)/shard_map/ppermute | solution.py:8
  113.5 9.8 %collective-permute-start.8 = (bf16[2,1,4,64,128]{4,3,2,1,0:T(8,128)(2,1)S(1)}, bf16[2,1,4,64,128]{4,3,2,1,0:T(8,128)(2,1)S(1)}, u32[]{:S(2)}, u32[]{:S(2)}) collective-permute-start(bf16[2,1,4,64,128]{4,3,2,1,0:T(8,128)(2,1)S(1)} %constant_dynamic-slice_fusion.49), channel_id=1, source_target_pairs={{0,8},{1,9},{2,10},{3,11},{4,12},{5,13},{6,14},{7,15},{8,0},{9,1},... | collective-permute-start | bytes 393224 | tf_op jit(solution)/shard_map/ppermute | solution.py:8
  123.4 5.1 collective-permute-start.9
  128.5 7.4 %collective-permute-start.10 = (bf16[16,64,128]{2,1,0:T(8,128)(2,1)S(1)}, bf16[16,64,128]{2,1,0:T(8,128)(2,1)S(1)}, u32[]{:S(2)}, u32[]{:S(2)}) collective-permute-start(bf16[16,64,128]{2,1,0:T(8,128)(2,1)S(1)} %bitcast.363), channel_id=1, source_target_pairs={{0,64},{64,128},{128,192},{1,65},{65,129},{129,193},{2,66},{66,130... | collective-permute-start | bytes 786440 | tf_op jit(solution)/shard_map/ppermute | solution.py:14
  152.6 7.5 %collective-permute-start.13 = (bf16[4,1,2,64,128]{4,3,2,1,0:T(8,128)(2,1)S(1)}, bf16[4,1,2,64,128]{4,3,2,1,0:T(8,128)(2,1)S(1)}, u32[]{:S(2)}, u32[]{:S(2)}) collective-permute-start(bf16[4,1,2,64,128]{4,3,2,1,0:T(8,128)(2,1)S(1)} %constant_dynamic-slice_fusion.46), channel_id=1, source_target_pairs={{0,4},{1,5},{2,6},{3,7},{4,0},{5,1},{6,2},{7,3},{8,12},{9,13},{10,... | collective-permute-start | bytes 393224 | tf_op jit(solution)/shard_map/ppermute | solution.py:8
  160.1 11.3 %collective-permute-start.14 = (bf16[2,1,4,64,128]{4,3,2,1,0:T(8,128)(2,1)S(1)}, bf16[2,1,4,64,128]{4,3,2,1,0:T(8,128)(2,1)S(1)}, u32[]{:S(2)}, u32[]{:S(2)}) collective-permute-start(bf16[2,1,4,64,128]{4,3,2,1,0:T(8,128)(2,1)S(1)} %constant_dynamic-slice_fusion.45), channel_id=1, source_target_pairs={{0,8},{1,9},{2,10},{3,11},{4,12},{5,13},{6,14},{7,15},{8,0},{9,1},... | collective-permute-start | bytes 393224 | tf_op jit(solution)/shard_map/ppermute | solution.py:8
  171.4 5.2 collective-permute-start.15
  176.6 9.0 %collective-permute-start.16 = (bf16[16,64,128]{2,1,0:T(8,128)(2,1)S(1)}, bf16[16,64,128]{2,1,0:T(8,128)(2,1)S(1)}, u32[]{:S(2)}, u32[]{:S(2)}) collective-permute-start(bf16[16,64,128]{2,1,0:T(8,128)(2,1)S(1)} %bitcast.372), channel_id=1, source_target_pairs={{0,32},{1,33},{2,34},{3,35},{4,36},{5,37},{6,38},{7,39},{8,40},{9,... | collective-permute-start | bytes 786440 | tf_op jit(solution)/shard_map/ppermute | solution.py:8
  197.0 7.1 %collective-permute-start.18 = (bf16[4,1,2,64,128]{4,3,2,1,0:T(8,128)(2,1)S(1)}, bf16[4,1,2,64,128]{4,3,2,1,0:T(8,128)(2,1)S(1)}, u32[]{:S(2)}, u32[]{:S(2)}) collective-permute-start(bf16[4,1,2,64,128]{4,3,2,1,0:T(8,128)(2,1)S(1)} %constant_dynamic-slice_fusion.42), channel_id=1, source_target_pairs={{0,4},{1,5},{2,6},{3,7},{4,0},{5,1},{6,2},{7,3},{8,12},{9,13},{10,... | collective-permute-start | bytes 393224 | tf_op jit(solution)/shard_map/ppermute | solution.py:8
  204.1 10.4 %collective-permute-start.19 = (bf16[2,1,4,64,128]{4,3,2,1,0:T(8,128)(2,1)S(1)}, bf16[2,1,4,64,128]{4,3,2,1,0:T(8,128)(2,1)S(1)}, u32[]{:S(2)}, u32[]{:S(2)}) collective-permute-start(bf16[2,1,4,64,128]{4,3,2,1,0:T(8,128)(2,1)S(1)} %constant_dynamic-slice_fusion.41), channel_id=1, source_target_pairs={{0,8},{1,9},{2,10},{3,11},{4,12},{5,13},{6,14},{7,15},{8,0},{9,1},... | collective-permute-start | bytes 393224 | tf_op jit(solution)/shard_map/ppermute | solution.py:8
  214.5 5.1 collective-permute-start.20
  219.6 8.3 %collective-permute-start.21 = (bf16[16,64,128]{2,1,0:T(8,128)(2,1)S(1)}, bf16[16,64,128]{2,1,0:T(8,128)(2,1)S(1)}, u32[]{:S(2)}, u32[]{:S(2)}) collective-permute-start(bf16[16,64,128]{2,1,0:T(8,128)(2,1)S(1)} %bitcast.382), channel_id=1, source_target_pairs={{0,64},{64,128},{128,192},{1,65},{65,129},{129,193},{2,66},{66,130... | collective-permute-start | bytes 786440 | tf_op jit(solution)/shard_map/ppermute | solution.py:14
  235.8 5.6 collective-permute-start.23
  241.5 8.5 %collective-permute-start.24 = (bf16[4,1,2,64,128]{4,3,2,1,0:T(8,128)(2,1)S(1)}, bf16[4,1,2,64,128]{4,3,2,1,0:T(8,128)(2,1)S(1)}, u32[]{:S(2)}, u32[]{:S(2)}) collective-permute-start(bf16[4,1,2,64,128]{4,3,2,1,0:T(8,128)(2,1)S(1)} %constant_dynamic-slice_fusion.38), channel_id=1, source_target_pairs={{0,4},{1,5},{2,6},{3,7},{4,0},{5,1},{6,2},{7,3},{8,12},{9,13},{10,... | collective-permute-start | bytes 393224 | tf_op jit(solution)/shard_map/ppermute | solution.py:8
  250.0 11.8 %collective-permute-start.25 = (bf16[2,1,4,64,128]{4,3,2,1,0:T(8,128)(2,1)S(1)}, bf16[2,1,4,64,128]{4,3,2,1,0:T(8,128)(2,1)S(1)}, u32[]{:S(2)}, u32[]{:S(2)}) collective-permute-start(bf16[2,1,4,64,128]{4,3,2,1,0:T(8,128)(2,1)S(1)} %constant_dynamic-slice_fusion.37), channel_id=1, source_target_pairs={{0,8},{1,9},{2,10},{3,11},{4,12},{5,13},{6,14},{7,15},{8,0},{9,1},... | collective-permute-start | bytes 393224 | tf_op jit(solution)/shard_map/ppermute | solution.py:8
  261.9 5.5 collective-permute-start.26
  267.4 9.2 %collective-permute-start.27 = (bf16[16,64,128]{2,1,0:T(8,128)(2,1)S(1)}, bf16[16,64,128]{2,1,0:T(8,128)(2,1)S(1)}, u32[]{:S(2)}, u32[]{:S(2)}) collective-permute-start(bf16[16,64,128]{2,1,0:T(8,128)(2,1)S(1)} %bitcast.391), channel_id=1, source_target_pairs={{0,32},{1,33},{2,34},{3,35},{4,36},{5,37},{6,38},{7,39},{8,40},{9,... | collective-permute-start | bytes 786440 | tf_op jit(solution)/shard_map/ppermute | solution.py:8
  282.8 5.1 collective-permute-start.28
  287.9 6.9 collective-permute-start.29
  294.8 10.3 %collective-permute-start.30 = (bf16[2,1,4,64,128]{4,3,2,1,0:T(8,128)(2,1)S(1)}, bf16[2,1,4,64,128]{4,3,2,1,0:T(8,128)(2,1)S(1)}, u32[]{:S(2)}, u32[]{:S(2)}) collective-permute-start(bf16[2,1,4,64,128]{4,3,2,1,0:T(8,128)(2,1)S(1)} %constant_dynamic-slice_fusion.33), channel_id=1, source_target_pairs={{0,8},{1,9},{2,10},{3,11},{4,12},{5,13},{6,14},{7,15},{8,0},{9,1},... | collective-permute-start | bytes 393224 | tf_op jit(solution)/shard_map/ppermute | solution.py:8
  310.2 8.3 %collective-permute-start.32 = (bf16[16,64,128]{2,1,0:T(8,128)(2,1)S(1)}, bf16[16,64,128]{2,1,0:T(8,128)(2,1)S(1)}, u32[]{:S(2)}, u32[]{:S(2)}) collective-permute-start(bf16[16,64,128]{2,1,0:T(8,128)(2,1)S(1)} %bitcast.401), channel_id=1, source_target_pairs={{0,64},{64,128},{128,192},{1,65},{65,129},{129,193},{2,66},{66,130... | collective-permute-start | bytes 786440 | tf_op jit(solution)/shard_map/ppermute | solution.py:14
  326.7 5.6 collective-permute-start.34
  332.4 8.5 %collective-permute-start.35 = (bf16[4,1,2,64,128]{4,3,2,1,0:T(8,128)(2,1)S(1)}, bf16[4,1,2,64,128]{4,3,2,1,0:T(8,128)(2,1)S(1)}, u32[]{:S(2)}, u32[]{:S(2)}) collective-permute-start(bf16[4,1,2,64,128]{4,3,2,1,0:T(8,128)(2,1)S(1)} %constant_dynamic-slice_fusion.30), channel_id=1, source_target_pairs={{0,4},{1,5},{2,6},{3,7},{4,0},{5,1},{6,2},{7,3},{8,12},{9,13},{10,... | collective-permute-start | bytes 393224 | tf_op jit(solution)/shard_map/ppermute | solution.py:8
  340.9 11.8 %collective-permute-start.36 = (bf16[2,1,4,64,128]{4,3,2,1,0:T(8,128)(2,1)S(1)}, bf16[2,1,4,64,128]{4,3,2,1,0:T(8,128)(2,1)S(1)}, u32[]{:S(2)}, u32[]{:S(2)}) collective-permute-start(bf16[2,1,4,64,128]{4,3,2,1,0:T(8,128)(2,1)S(1)} %constant_dynamic-slice_fusion.29), channel_id=1, source_target_pairs={{0,8},{1,9},{2,10},{3,11},{4,12},{5,13},{6,14},{7,15},{8,0},{9,1},... | collective-permute-start | bytes 393224 | tf_op jit(solution)/shard_map/ppermute | solution.py:8
  352.8 5.5 collective-permute-start.37
  358.3 9.1 %collective-permute-start.38 = (bf16[16,64,128]{2,1,0:T(8,128)(2,1)S(1)}, bf16[16,64,128]{2,1,0:T(8,128)(2,1)S(1)}, u32[]{:S(2)}, u32[]{:S(2)}) collective-permute-start(bf16[16,64,128]{2,1,0:T(8,128)(2,1)S(1)} %bitcast.410), channel_id=1, source_target_pairs={{0,32},{1,33},{2,34},{3,35},{4,36},{5,37},{6,38},{7,39},{8,40},{9,... | collective-permute-start | bytes 786440 | tf_op jit(solution)/shard_map/ppermute | solution.py:8
  373.7 5.1 collective-permute-start.39
  378.8 6.9 collective-permute-start.40
  385.7 10.3 %collective-permute-start.41 = (bf16[2,1,4,64,128]{4,3,2,1,0:T(8,128)(2,1)S(1)}, bf16[2,1,4,64,128]{4,3,2,1,0:T(8,128)(2,1)S(1)}, u32[]{:S(2)}, u32[]{:S(2)}) collective-permute-start(bf16[2,1,4,64,128]{4,3,2,1,0:T(8,128)(2,1)S(1)} %constant_dynamic-slice_fusion.25), channel_id=1, source_target_pairs={{0,8},{1,9},{2,10},{3,11},{4,12},{5,13},{6,14},{7,15},{8,0},{9,1},... | collective-permute-start | bytes 393224 | tf_op jit(solution)/shard_map/ppermute | solution.py:8
  401.1 8.3 %collective-permute-start.43 = (bf16[16,64,128]{2,1,0:T(8,128)(2,1)S(1)}, bf16[16,64,128]{2,1,0:T(8,128)(2,1)S(1)}, u32[]{:S(2)}, u32[]{:S(2)}) collective-permute-start(bf16[16,64,128]{2,1,0:T(8,128)(2,1)S(1)} %bitcast.303), channel_id=1, source_target_pairs={{0,64},{64,128},{128,192},{1,65},{65,129},{129,193},{2,66},{66,130... | collective-permute-start | bytes 786440 | tf_op jit(solution)/shard_map/ppermute | solution.py:14
  417.4 5.6 collective-permute-start.45
  423.1 8.5 %collective-permute-start.46 = (bf16[4,1,2,64,128]{4,3,2,1,0:T(8,128)(2,1)S(1)}, bf16[4,1,2,64,128]{4,3,2,1,0:T(8,128)(2,1)S(1)}, u32[]{:S(2)}, u32[]{:S(2)}) collective-permute-start(bf16[4,1,2,64,128]{4,3,2,1,0:T(8,128)(2,1)S(1)} %constant_dynamic-slice_fusion.22), channel_id=1, source_target_pairs={{0,4},{1,5},{2,6},{3,7},{4,0},{5,1},{6,2},{7,3},{8,12},{9,13},{10,... | collective-permute-start | bytes 393224 | tf_op jit(solution)/shard_map/ppermute | solution.py:8
  431.6 11.8 %collective-permute-start.47 = (bf16[2,1,4,64,128]{4,3,2,1,0:T(8,128)(2,1)S(1)}, bf16[2,1,4,64,128]{4,3,2,1,0:T(8,128)(2,1)S(1)}, u32[]{:S(2)}, u32[]{:S(2)}) collective-permute-start(bf16[2,1,4,64,128]{4,3,2,1,0:T(8,128)(2,1)S(1)} %constant_dynamic-slice_fusion.21), channel_id=1, source_target_pairs={{0,8},{1,9},{2,10},{3,11},{4,12},{5,13},{6,14},{7,15},{8,0},{9,1},... | collective-permute-start | bytes 393224 | tf_op jit(solution)/shard_map/ppermute | solution.py:8
  443.5 5.5 collective-permute-start.48
  449.0 9.4 %collective-permute-start.49 = (bf16[16,64,128]{2,1,0:T(8,128)(2,1)S(1)}, bf16[16,64,128]{2,1,0:T(8,128)(2,1)S(1)}, u32[]{:S(2)}, u32[]{:S(2)}) collective-permute-start(bf16[16,64,128]{2,1,0:T(8,128)(2,1)S(1)} %bitcast.420), channel_id=1, source_target_pairs={{0,32},{1,33},{2,34},{3,35},{4,36},{5,37},{6,38},{7,39},{8,40},{9,... | collective-permute-start | bytes 786440 | tf_op jit(solution)/shard_map/ppermute | solution.py:8
  469.7 6.9 collective-permute-start.51
  476.6 10.3 %collective-permute-start.52 = (bf16[2,1,4,64,128]{4,3,2,1,0:T(8,128)(2,1)S(1)}, bf16[2,1,4,64,128]{4,3,2,1,0:T(8,128)(2,1)S(1)}, u32[]{:S(2)}, u32[]{:S(2)}) collective-permute-start(bf16[2,1,4,64,128]{4,3,2,1,0:T(8,128)(2,1)S(1)} %constant_dynamic-slice_fusion.17), channel_id=1, source_target_pairs={{0,8},{1,9},{2,10},{3,11},{4,12},{5,13},{6,14},{7,15},{8,0},{9,1},... | collective-permute-start | bytes 393224 | tf_op jit(solution)/shard_map/ppermute | solution.py:8
  487.0 5.1 collective-permute-start.53
  492.0 8.3 %collective-permute-start.54 = (bf16[16,64,128]{2,1,0:T(8,128)(2,1)S(1)}, bf16[16,64,128]{2,1,0:T(8,128)(2,1)S(1)}, u32[]{:S(2)}, u32[]{:S(2)}) collective-permute-start(bf16[16,64,128]{2,1,0:T(8,128)(2,1)S(1)} %bitcast.322), channel_id=1, source_target_pairs={{0,64},{64,128},{128,192},{1,65},{65,129},{129,193},{2,66},{66,130... | collective-permute-start | bytes 786440 | tf_op jit(solution)/shard_map/ppermute | solution.py:14
  508.3 5.6 collective-permute-start.56
  514.0 8.5 %collective-permute-start.57 = (bf16[4,1,2,64,128]{4,3,2,1,0:T(8,128)(2,1)S(1)}, bf16[4,1,2,64,128]{4,3,2,1,0:T(8,128)(2,1)S(1)}, u32[]{:S(2)}, u32[]{:S(2)}) collective-permute-start(bf16[4,1,2,64,128]{4,3,2,1,0:T(8,128)(2,1)S(1)} %constant_dynamic-slice_fusion.14), channel_id=1, source_target_pairs={{0,4},{1,5},{2,6},{3,7},{4,0},{5,1},{6,2},{7,3},{8,12},{9,13},{10,... | collective-permute-start | bytes 393224 | tf_op jit(solution)/shard_map/ppermute | solution.py:8
  522.5 11.8 %collective-permute-start.58 = (bf16[2,1,4,64,128]{4,3,2,1,0:T(8,128)(2,1)S(1)}, bf16[2,1,4,64,128]{4,3,2,1,0:T(8,128)(2,1)S(1)}, u32[]{:S(2)}, u32[]{:S(2)}) collective-permute-start(bf16[2,1,4,64,128]{4,3,2,1,0:T(8,128)(2,1)S(1)} %constant_dynamic-slice_fusion.13), channel_id=1, source_target_pairs={{0,8},{1,9},{2,10},{3,11},{4,12},{5,13},{6,14},{7,15},{8,0},{9,1},... | collective-permute-start | bytes 393224 | tf_op jit(solution)/shard_map/ppermute | solution.py:8
  534.4 5.5 collective-permute-start.59
  539.9 9.2 %collective-permute-start.60 = (bf16[16,64,128]{2,1,0:T(8,128)(2,1)S(1)}, bf16[16,64,128]{2,1,0:T(8,128)(2,1)S(1)}, u32[]{:S(2)}, u32[]{:S(2)}) collective-permute-start(bf16[16,64,128]{2,1,0:T(8,128)(2,1)S(1)} %bitcast.430), channel_id=1, source_target_pairs={{0,32},{1,33},{2,34},{3,35},{4,36},{5,37},{6,38},{7,39},{8,40},{9,... | collective-permute-start | bytes 786440 | tf_op jit(solution)/shard_map/ppermute | solution.py:8
  555.2 5.1 collective-permute-start.61
  560.3 6.9 collective-permute-start.62
  567.3 10.3 %collective-permute-start.63 = (bf16[2,1,4,64,128]{4,3,2,1,0:T(8,128)(2,1)S(1)}, bf16[2,1,4,64,128]{4,3,2,1,0:T(8,128)(2,1)S(1)}, u32[]{:S(2)}, u32[]{:S(2)}) collective-permute-start(bf16[2,1,4,64,128]{4,3,2,1,0:T(8,128)(2,1)S(1)} %constant_dynamic-slice_fusion.9), channel_id=1, source_target_pairs={{0,8},{1,9},{2,10},{3,11},{4,12},{5,13},{6,14},{7,15},{8,0},{9,1},... | collective-permute-start | bytes 393224 | tf_op jit(solution)/shard_map/ppermute | solution.py:8
  577.6 5.1 collective-permute-start.64
  582.7 8.3 %collective-permute-start.65 = (bf16[16,64,128]{2,1,0:T(8,128)(2,1)S(1)}, bf16[16,64,128]{2,1,0:T(8,128)(2,1)S(1)}, u32[]{:S(2)}, u32[]{:S(2)}) collective-permute-start(bf16[16,64,128]{2,1,0:T(8,128)(2,1)S(1)} %bitcast.332), channel_id=1, source_target_pairs={{0,64},{64,128},{128,192},{1,65},{65,129},{129,193},{2,66},{66,130... | collective-permute-start | bytes 786440 | tf_op jit(solution)/shard_map/ppermute | solution.py:14
  599.2 5.6 collective-permute-start.67
  604.9 8.5 %collective-permute-start.68 = (bf16[4,1,2,64,128]{4,3,2,1,0:T(8,128)(2,1)S(1)}, bf16[4,1,2,64,128]{4,3,2,1,0:T(8,128)(2,1)S(1)}, u32[]{:S(2)}, u32[]{:S(2)}) collective-permute-start(bf16[4,1,2,64,128]{4,3,2,1,0:T(8,128)(2,1)S(1)} %constant_dynamic-slice_fusion.6), channel_id=1, source_target_pairs={{0,4},{1,5},{2,6},{3,7},{4,0},{5,1},{6,2},{7,3},{8,12},{9,13},{10,... | collective-permute-start | bytes 393224 | tf_op jit(solution)/shard_map/ppermute | solution.py:8
  613.4 11.8 %collective-permute-start.69 = (bf16[2,1,4,64,128]{4,3,2,1,0:T(8,128)(2,1)S(1)}, bf16[2,1,4,64,128]{4,3,2,1,0:T(8,128)(2,1)S(1)}, u32[]{:S(2)}, u32[]{:S(2)}) collective-permute-start(bf16[2,1,4,64,128]{4,3,2,1,0:T(8,128)(2,1)S(1)} %constant_dynamic-slice_fusion.5), channel_id=1, source_target_pairs={{0,8},{1,9},{2,10},{3,11},{4,12},{5,13},{6,14},{7,15},{8,0},{9,1},... | collective-permute-start | bytes 393224 | tf_op jit(solution)/shard_map/ppermute | solution.py:8
  625.3 5.5 collective-permute-start.70
  630.8 9.1 %collective-permute-start.71 = (bf16[16,64,128]{2,1,0:T(8,128)(2,1)S(1)}, bf16[16,64,128]{2,1,0:T(8,128)(2,1)S(1)}, u32[]{:S(2)}, u32[]{:S(2)}) collective-permute-start(bf16[16,64,128]{2,1,0:T(8,128)(2,1)S(1)} %bitcast.353), channel_id=1, source_target_pairs={{0,32},{1,33},{2,34},{3,35},{4,36},{5,37},{6,38},{7,39},{8,40},{9,... | collective-permute-start | bytes 786440 | tf_op jit(solution)/shard_map/ppermute | solution.py:8
  651.2 6.9 collective-permute-start.73
  658.2 10.3 %collective-permute-start.74 = (bf16[2,1,4,64,128]{4,3,2,1,0:T(8,128)(2,1)S(1)}, bf16[2,1,4,64,128]{4,3,2,1,0:T(8,128)(2,1)S(1)}, u32[]{:S(2)}, u32[]{:S(2)}) collective-permute-start(bf16[2,1,4,64,128]{4,3,2,1,0:T(8,128)(2,1)S(1)} %constant_dynamic-slice_fusion.1), channel_id=1, source_target_pairs={{0,8},{1,9},{2,10},{3,11},{4,12},{5,13},{6,14},{7,15},{8,0},{9,1},... | collective-permute-start | bytes 393224 | tf_op jit(solution)/shard_map/ppermute | solution.py:8
  668.5 5.1 collective-permute-start.75
  (19 other events, 306.4 us)
where the time goes:
time: 700 us; the launch traced here: 690 us
  waiting for transfers between devices  428 us (61%)
  matrix products  114 us (16%)
  starting transfers between devices  94.7 us (14%)
  local copies, waits for them, and re-layouts  35 us (5%)
  blocking collectives  15.9 us (2%)
    ppermute x70, waiting for transfers between devices, from_partner(): lax.ppermute(array, axis, [(i, i ^ 1 << stride) for i in range(lax.axis_s...  405 us
    dot_general x14, matrix products, apply_layer(): summed = jnp.dot(matrix, flat_group, preferred_element_type=jnp.float32)  96 us
    ppermute x70, starting transfers between devices, from_partner(): lax.ppermute(array, axis, [(i, i ^ 1 << stride) for i in range(lax.axis_s...  69.2 us
    another operation x2, local copies, waits for them, and re-layouts, permuted_weights(): weights.reshape(blocks, tile_size, fan_count, row_width // fan_count)  25.7 us
    ppermute x6, starting transfers between devices, passed_along(): lax.ppermute(value, axis, [(source, source + steps) for source in range(i...  25.5 us
    ppermute x6, waiting for transfers between devices, passed_along(): lax.ppermute(value, axis, [(source, source + steps) for source in range(i...  23.1 us
    dot_general x2, matrix products, permuted_weights(): jnp.einsum('jakc,jkm->jamc', shaped, onehot, preferred_element_type=jnp.f...  18.1 us
    all_to_all x1, blocking collectives, body(): lax.all_to_all(results[:, None], 'segment', split_axis=0, concat_axis=1,...  15.9 us
  transfers between devices with their start and end apart: 76, of which 73 were waited for; matrix products, arithmetic and copies ran while one was open for 7% of the time, Pallas kernels for 0%

commit v1 on v0

--- a/solution.py
+++ b/solution.py
@@ -83,7 +83,15 @@
             results = results.at[finished].set(present)
         if step_index + 1 < step_count:
             arriving = passed_along(present, "segment", 1)
-    gathered = lax.all_to_all(results[:, None], "segment", split_axis=0, concat_axis=1, tiled=True)
+    gathered = jnp.concatenate(
+        lax.all_to_all(
+            jnp.stack(jnp.split(results[:, None], lax.axis_size("segment"), axis=0)),
+            "segment",
+            0,
+            0,
+        ),
+        axis=1,
+    )
     return gathered[:, segments - 1]
 
 

time: 700 us -> 700 us (level)
  no operation moved by 1% of the time
where the time goes in v1:
time: 700 us; the launch traced here: 691 us
  waiting for transfers between devices  428 us (61%)
  matrix products  114 us (16%)
  starting transfers between devices  94.7 us (14%)
  local copies, waits for them, and re-layouts  34.7 us (5%)
  blocking collectives  15.9 us (2%)
    ppermute x70, waiting for transfers between devices, from_partner(): lax.ppermute(array, axis, [(i, i ^ 1 << stride) for i in range(lax.axis_s...  405 us
    dot_general x14, matrix products, apply_layer(): summed = jnp.dot(matrix, flat_group, preferred_element_type=jnp.float32)  96 us
    ppermute x70, starting transfers between devices, from_partner(): lax.ppermute(array, axis, [(i, i ^ 1 << stride) for i in range(lax.axis_s...  69.2 us
    another operation x2, local copies, waits for them, and re-layouts, permuted_weights(): weights.reshape(blocks, tile_size, fan_count, row_width // fan_count)  25.7 us
    ppermute x6, starting transfers between devices, passed_along(): lax.ppermute(value, axis, [(source, source + steps) for source in range(i...  25.5 us
    ppermute x6, waiting for transfers between devices, passed_along(): lax.ppermute(value, axis, [(source, source + steps) for source in range(i...  23.1 us
    dot_general x2, matrix products, permuted_weights(): jnp.einsum('jakc,jkm->jamc', shaped, onehot, preferred_element_type=jnp.f...  18.1 us
    all_to_all x1, blocking collectives, body(): lax.all_to_all(jnp.stack(jnp.split(results[:, None], lax.axis_size('segme...  15.9 us
  transfers between devices with their start and end apart: 76, of which 73 were waited for; matrix products, arithmetic and copies ran while one was open for 7% of the time, Pallas kernels for 0%

profile of v1, /device:TPU:96, one launch (start us, length us, event | category | flops | bytes accessed | tf_op | source)
XLA Modules:
  0.0 690.6 jit_solution(12734978153139314345)
XLA Ops:
  1.1 6.3 fusion.328
  7.4 12.9 %reshape_squeeze.7 = bf16[16,64,32,64]{3,2,1,0:T(8,128)(2,1)} reshape(bf16[1,16,64,2048]{3,2,1,0:T(8,128)(2,1)} %get-tuple-element.53) | data formatting | bytes 8388608 | tf_op jit(solution)/shard_map/reshape;squeeze | solution.py:20
  20.3 9.1 %convert_bitcast_fusion = bf16[16,64,32,64]{3,2,1,0:T(8,128)(2,1)} fusion(bf16[16,64,32,64]{3,2,1,0:T(8,128)(2,1)} %reshape_squeeze.7, s32[16,32]{1,0:T(8,128)S(1)} %get-tuple-element.57), kind=kOutput, calls=%fused_computation | convolution fusion | flops 136331264 | bytes 8390656 | tf_op jit(solution)/shard_map/jakc,jkm->jamc/dot_general | solution.py:24
  29.3 9.2 %fusion.163 = bf16[16,64,128]{2,1,0:T(8,128)(2,1)S(1)} fusion(bf16[16,64,32,64]{3,2,1,0:T(8,128)(2,1)} %convert_bitcast_fusion, bf16[16,64,128]{2,1,0:T(8,128)(2,1)S(1)} %collective-permute-done, bf16[16,64,128]{2,1,0:T(8,128)(2,1)S(1)} %select_bitcast_fusion, pred[]{:T(512)S(6)} %eq.137, f32[16,64]{1,0:T(8,128)S(1)} %get-tuple-element.56), kind=kOutput, calls=%fused_computation.75 | convolution fusion | flops 538050560 | bytes 4984833 | tf_op jit(solution)/shard_map/dot_general | solution.py:40
  38.8 5.8 collective-permute-done.1
  44.7 8.6 %collective-permute-done.2 = bf16[4,1,2,64,128]{4,3,2,1,0:T(8,128)(2,1)S(1)} collective-permute-done((bf16[4,1,2,64,128]{4,3,2,1,0:T(8,128)(2,1)S(1)}, bf16[4,1,2,64,128]{4,3,2,1,0:T(8,128)(2,1)S(1)}, u32[]{:S(2)}, u32[]{:S(2)}) %collective-permute-start.2) | collective-permute-done | bytes 131104 | tf_op jit(solution)/shard_map/ppermute | solution.py:8
  58.2 7.5 %collective-permute-done.3 = bf16[2,1,4,64,128]{4,3,2,1,0:T(8,128)(2,1)S(1)} collective-permute-done((bf16[2,1,4,64,128]{4,3,2,1,0:T(8,128)(2,1)S(1)}, bf16[2,1,4,64,128]{4,3,2,1,0:T(8,128)(2,1)S(1)}, u32[]{:S(2)}, u32[]{:S(2)}) %collective-permute-start.3) | collective-permute-done | bytes 131104 | tf_op jit(solution)/shard_map/ppermute | solution.py:8
  67.4 12.9 %reshape_squeeze.6 = bf16[16,64,32,64]{3,2,1,0:T(8,128)(2,1)} reshape(bf16[1,16,64,2048]{3,2,1,0:T(8,128)(2,1)} %get-tuple-element.54) | data formatting | bytes 8388608 | tf_op jit(solution)/shard_map/reshape;squeeze | solution.py:20
  83.1 9.0 %convert_bitcast_fusion.1 = bf16[16,64,32,64]{3,2,1,0:T(8,128)(2,1)} fusion(bf16[16,64,32,64]{3,2,1,0:T(8,128)(2,1)} %reshape_squeeze.6, s32[16,32]{1,0:T(8,128)S(1)} %get-tuple-element.58), kind=kOutput, calls=%fused_computation.1 | convolution fusion | flops 136331264 | bytes 8390656 | tf_op jit(solution)/shard_map/jakc,jkm->jamc/dot_general | solution.py:24
  92.1 9.2 %fusion.184 = bf16[16,64,128]{2,1,0:T(8,128)(2,1)S(1)} fusion(bf16[16,64,32,64]{3,2,1,0:T(8,128)(2,1)} %convert_bitcast_fusion.1, bf16[16,64,128]{2,1,0:T(8,128)(2,1)S(1)} %collective-permute-done.5, bf16[16,64,128]{2,1,0:T(8,128)(2,1)S(1)} %bitcast.336, pred[]{:T(512)S(6)} %eq.132, f32[16,64]{1,0:T(8,128)S(1)} %get-tuple-element.55), kind=kOutput, calls=%fused_computation.82 | convolution fusion | flops 538050560 | bytes 4984833 | tf_op jit(solution)/shard_map/dot_general | solution.py:40
  101.5 5.0 collective-permute-done.6
  106.8 6.7 collective-permute-done.7
  116.8 6.5 collective-permute-done.8
  137.5 10.0 %fusion.160 = bf16[16,64,128]{2,1,0:T(8,128)(2,1)S(1)} fusion(bf16[16,64,32,64]{3,2,1,0:T(8,128)(2,1)} %convert_bitcast_fusion, bf16[16,64,128]{2,1,0:T(8,128)(2,1)S(1)} %collective-permute-done.11, bf16[16,64,128]{2,1,0:T(8,128)(2,1)S(1)} %bitcast_select_fusion, pred[]{:T(512)S(6)} %eq.137, f32[16,64]{1,0:T(8,128)S(1)} %get-tuple-element.56), kind=kOutput, calls=%fused_computation.74 | convolution fusion | flops 538050560 | bytes 4984833 | tf_op jit(solution)/shard_map/dot_general | solution.py:40
  152.9 7.2 %collective-permute-done.13 = bf16[4,1,2,64,128]{4,3,2,1,0:T(8,128)(2,1)S(1)} collective-permute-done((bf16[4,1,2,64,128]{4,3,2,1,0:T(8,128)(2,1)S(1)}, bf16[4,1,2,64,128]{4,3,2,1,0:T(8,128)(2,1)S(1)}, u32[]{:S(2)}, u32[]{:S(2)}) %collective-permute-start.13) | collective-permute-done | bytes 131104 | tf_op jit(solution)/shard_map/ppermute | solution.py:8
  163.5 7.9 %collective-permute-done.14 = bf16[2,1,4,64,128]{4,3,2,1,0:T(8,128)(2,1)S(1)} collective-permute-done((bf16[2,1,4,64,128]{4,3,2,1,0:T(8,128)(2,1)S(1)}, bf16[2,1,4,64,128]{4,3,2,1,0:T(8,128)(2,1)S(1)}, u32[]{:S(2)}, u32[]{:S(2)}) %collective-permute-start.14) | collective-permute-done | bytes 131104 | tf_op jit(solution)/shard_map/ppermute | solution.py:8
  177.9 7.8 %collective-permute-done.16 = bf16[16,64,128]{2,1,0:T(8,128)(2,1)S(1)} collective-permute-done((bf16[16,64,128]{2,1,0:T(8,128)(2,1)S(1)}, bf16[16,64,128]{2,1,0:T(8,128)(2,1)S(1)}, u32[]{:S(2)}, u32[]{:S(2)}) %collective-permute-start.16) | collective-permute-done | bytes 262176 | tf_op jit(solution)/shard_map/ppermute | solution.py:8
  185.7 6.2 fusion.181
  197.1 7.0 %collective-permute-done.18 = bf16[4,1,2,64,128]{4,3,2,1,0:T(8,128)(2,1)S(1)} collective-permute-done((bf16[4,1,2,64,128]{4,3,2,1,0:T(8,128)(2,1)S(1)}, bf16[4,1,2,64,128]{4,3,2,1,0:T(8,128)(2,1)S(1)}, u32[]{:S(2)}, u32[]{:S(2)}) %collective-permute-start.18) | collective-permute-done | bytes 131104 | tf_op jit(solution)/shard_map/ppermute | solution.py:8
  208.5 5.9 collective-permute-done.19
  214.6 5.0 collective-permute-done.20
  229.7 6.2 fusion.157
  235.9 5.5 collective-permute-done.23
  241.6 8.4 %collective-permute-done.24 = bf16[4,1,2,64,128]{4,3,2,1,0:T(8,128)(2,1)S(1)} collective-permute-done((bf16[4,1,2,64,128]{4,3,2,1,0:T(8,128)(2,1)S(1)}, bf16[4,1,2,64,128]{4,3,2,1,0:T(8,128)(2,1)S(1)}, u32[]{:S(2)}, u32[]{:S(2)}) %collective-permute-start.24) | collective-permute-done | bytes 131104 | tf_op jit(solution)/shard_map/ppermute | solution.py:8
  253.1 8.8 %collective-permute-done.25 = bf16[2,1,4,64,128]{4,3,2,1,0:T(8,128)(2,1)S(1)} collective-permute-done((bf16[2,1,4,64,128]{4,3,2,1,0:T(8,128)(2,1)S(1)}, bf16[2,1,4,64,128]{4,3,2,1,0:T(8,128)(2,1)S(1)}, u32[]{:S(2)}, u32[]{:S(2)}) %collective-permute-start.25) | collective-permute-done | bytes 131104 | tf_op jit(solution)/shard_map/ppermute | solution.py:8
  262.0 5.4 collective-permute-done.26
  268.5 8.1 %collective-permute-done.27 = bf16[16,64,128]{2,1,0:T(8,128)(2,1)S(1)} collective-permute-done((bf16[16,64,128]{2,1,0:T(8,128)(2,1)S(1)}, bf16[16,64,128]{2,1,0:T(8,128)(2,1)S(1)}, u32[]{:S(2)}, u32[]{:S(2)}) %collective-permute-start.27) | collective-permute-done | bytes 262176 | tf_op jit(solution)/shard_map/ppermute | solution.py:8
  276.6 6.2 fusion.178
  282.9 5.0 collective-permute-done.28
  288.0 6.8 collective-permute-done.29
  297.9 7.3 %collective-permute-done.30 = bf16[2,1,4,64,128]{4,3,2,1,0:T(8,128)(2,1)S(1)} collective-permute-done((bf16[2,1,4,64,128]{4,3,2,1,0:T(8,128)(2,1)S(1)}, bf16[2,1,4,64,128]{4,3,2,1,0:T(8,128)(2,1)S(1)}, u32[]{:S(2)}, u32[]{:S(2)}) %collective-permute-start.30) | collective-permute-done | bytes 131104 | tf_op jit(solution)/shard_map/ppermute | solution.py:8
  320.6 6.2 fusion.154
  326.8 5.5 collective-permute-done.34
  332.5 8.4 %collective-permute-done.35 = bf16[4,1,2,64,128]{4,3,2,1,0:T(8,128)(2,1)S(1)} collective-permute-done((bf16[4,1,2,64,128]{4,3,2,1,0:T(8,128)(2,1)S(1)}, bf16[4,1,2,64,128]{4,3,2,1,0:T(8,128)(2,1)S(1)}, u32[]{:S(2)}, u32[]{:S(2)}) %collective-permute-start.35) | collective-permute-done | bytes 131104 | tf_op jit(solution)/shard_map/ppermute | solution.py:8
  344.0 8.8 %collective-permute-done.36 = bf16[2,1,4,64,128]{4,3,2,1,0:T(8,128)(2,1)S(1)} collective-permute-done((bf16[2,1,4,64,128]{4,3,2,1,0:T(8,128)(2,1)S(1)}, bf16[2,1,4,64,128]{4,3,2,1,0:T(8,128)(2,1)S(1)}, u32[]{:S(2)}, u32[]{:S(2)}) %collective-permute-start.36) | collective-permute-done | bytes 131104 | tf_op jit(solution)/shard_map/ppermute | solution.py:8
  359.4 8.1 %collective-permute-done.38 = bf16[16,64,128]{2,1,0:T(8,128)(2,1)S(1)} collective-permute-done((bf16[16,64,128]{2,1,0:T(8,128)(2,1)S(1)}, bf16[16,64,128]{2,1,0:T(8,128)(2,1)S(1)}, u32[]{:S(2)}, u32[]{:S(2)}) %collective-permute-start.38) | collective-permute-done | bytes 262176 | tf_op jit(solution)/shard_map/ppermute | solution.py:8
  367.5 6.2 fusion.175
  378.9 6.8 collective-permute-done.40
  388.7 7.3 %collective-permute-done.41 = bf16[2,1,4,64,128]{4,3,2,1,0:T(8,128)(2,1)S(1)} collective-permute-done((bf16[2,1,4,64,128]{4,3,2,1,0:T(8,128)(2,1)S(1)}, bf16[2,1,4,64,128]{4,3,2,1,0:T(8,128)(2,1)S(1)}, u32[]{:S(2)}, u32[]{:S(2)}) %collective-permute-start.41) | collective-permute-done | bytes 131104 | tf_op jit(solution)/shard_map/ppermute | solution.py:8
  411.3 6.2 fusion.166
  417.5 5.5 collective-permute-done.45
  423.2 8.4 %collective-permute-done.46 = bf16[4,1,2,64,128]{4,3,2,1,0:T(8,128)(2,1)S(1)} collective-permute-done((bf16[4,1,2,64,128]{4,3,2,1,0:T(8,128)(2,1)S(1)}, bf16[4,1,2,64,128]{4,3,2,1,0:T(8,128)(2,1)S(1)}, u32[]{:S(2)}, u32[]{:S(2)}) %collective-permute-start.46) | collective-permute-done | bytes 131104 | tf_op jit(solution)/shard_map/ppermute | solution.py:8
  434.7 8.8 %collective-permute-done.47 = bf16[2,1,4,64,128]{4,3,2,1,0:T(8,128)(2,1)S(1)} collective-permute-done((bf16[2,1,4,64,128]{4,3,2,1,0:T(8,128)(2,1)S(1)}, bf16[2,1,4,64,128]{4,3,2,1,0:T(8,128)(2,1)S(1)}, u32[]{:S(2)}, u32[]{:S(2)}) %collective-permute-start.47) | collective-permute-done | bytes 131104 | tf_op jit(solution)/shard_map/ppermute | solution.py:8
  450.3 8.1 %collective-permute-done.49 = bf16[16,64,128]{2,1,0:T(8,128)(2,1)S(1)} collective-permute-done((bf16[16,64,128]{2,1,0:T(8,128)(2,1)S(1)}, bf16[16,64,128]{2,1,0:T(8,128)(2,1)S(1)}, u32[]{:S(2)}, u32[]{:S(2)}) %collective-permute-start.49) | collective-permute-done | bytes 262176 | tf_op jit(solution)/shard_map/ppermute | solution.py:8
  458.4 6.2 fusion.187
  469.8 6.8 collective-permute-done.51
  479.6 7.3 %collective-permute-done.52 = bf16[2,1,4,64,128]{4,3,2,1,0:T(8,128)(2,1)S(1)} collective-permute-done((bf16[2,1,4,64,128]{4,3,2,1,0:T(8,128)(2,1)S(1)}, bf16[2,1,4,64,128]{4,3,2,1,0:T(8,128)(2,1)S(1)}, u32[]{:S(2)}, u32[]{:S(2)}) %collective-permute-start.52) | collective-permute-done | bytes 131104 | tf_op jit(solution)/shard_map/ppermute | solution.py:8
  502.1 6.2 fusion.169
  508.4 5.5 collective-permute-done.56
  514.1 8.4 %collective-permute-done.57 = bf16[4,1,2,64,128]{4,3,2,1,0:T(8,128)(2,1)S(1)} collective-permute-done((bf16[4,1,2,64,128]{4,3,2,1,0:T(8,128)(2,1)S(1)}, bf16[4,1,2,64,128]{4,3,2,1,0:T(8,128)(2,1)S(1)}, u32[]{:S(2)}, u32[]{:S(2)}) %collective-permute-start.57) | collective-permute-done | bytes 131104 | tf_op jit(solution)/shard_map/ppermute | solution.py:8
  525.6 8.8 %collective-permute-done.58 = bf16[2,1,4,64,128]{4,3,2,1,0:T(8,128)(2,1)S(1)} collective-permute-done((bf16[2,1,4,64,128]{4,3,2,1,0:T(8,128)(2,1)S(1)}, bf16[2,1,4,64,128]{4,3,2,1,0:T(8,128)(2,1)S(1)}, u32[]{:S(2)}, u32[]{:S(2)}) %collective-permute-start.58) | collective-permute-done | bytes 131104 | tf_op jit(solution)/shard_map/ppermute | solution.py:8
  541.0 8.1 %collective-permute-done.60 = bf16[16,64,128]{2,1,0:T(8,128)(2,1)S(1)} collective-permute-done((bf16[16,64,128]{2,1,0:T(8,128)(2,1)S(1)}, bf16[16,64,128]{2,1,0:T(8,128)(2,1)S(1)}, u32[]{:S(2)}, u32[]{:S(2)}) %collective-permute-start.60) | collective-permute-done | bytes 262176 | tf_op jit(solution)/shard_map/ppermute | solution.py:8
  549.1 6.2 fusion.190
  560.4 6.8 collective-permute-done.62
  570.3 7.3 %collective-permute-done.63 = bf16[2,1,4,64,128]{4,3,2,1,0:T(8,128)(2,1)S(1)} collective-permute-done((bf16[2,1,4,64,128]{4,3,2,1,0:T(8,128)(2,1)S(1)}, bf16[2,1,4,64,128]{4,3,2,1,0:T(8,128)(2,1)S(1)}, u32[]{:S(2)}, u32[]{:S(2)}) %collective-permute-start.63) | collective-permute-done | bytes 131104 | tf_op jit(solution)/shard_map/ppermute | solution.py:8
  593.1 6.2 fusion.172
  599.3 5.5 collective-permute-done.67
  605.0 8.4 %collective-permute-done.68 = bf16[4,1,2,64,128]{4,3,2,1,0:T(8,128)(2,1)S(1)} collective-permute-done((bf16[4,1,2,64,128]{4,3,2,1,0:T(8,128)(2,1)S(1)}, bf16[4,1,2,64,128]{4,3,2,1,0:T(8,128)(2,1)S(1)}, u32[]{:S(2)}, u32[]{:S(2)}) %collective-permute-start.68) | collective-permute-done | bytes 131104 | tf_op jit(solution)/shard_map/ppermute | solution.py:8
  616.5 8.8 %collective-permute-done.69 = bf16[2,1,4,64,128]{4,3,2,1,0:T(8,128)(2,1)S(1)} collective-permute-done((bf16[2,1,4,64,128]{4,3,2,1,0:T(8,128)(2,1)S(1)}, bf16[2,1,4,64,128]{4,3,2,1,0:T(8,128)(2,1)S(1)}, u32[]{:S(2)}, u32[]{:S(2)}) %collective-permute-start.69) | collective-permute-done | bytes 131104 | tf_op jit(solution)/shard_map/ppermute | solution.py:8
  631.8 8.1 %collective-permute-done.71 = bf16[16,64,128]{2,1,0:T(8,128)(2,1)S(1)} collective-permute-done((bf16[16,64,128]{2,1,0:T(8,128)(2,1)S(1)}, bf16[16,64,128]{2,1,0:T(8,128)(2,1)S(1)}, u32[]{:S(2)}, u32[]{:S(2)}) %collective-permute-start.71) | collective-permute-done | bytes 262176 | tf_op jit(solution)/shard_map/ppermute | solution.py:8
  639.9 6.2 fusion.193
  651.3 6.8 collective-permute-done.73
  661.2 7.3 %collective-permute-done.74 = bf16[2,1,4,64,128]{4,3,2,1,0:T(8,128)(2,1)S(1)} collective-permute-done((bf16[2,1,4,64,128]{4,3,2,1,0:T(8,128)(2,1)S(1)}, bf16[2,1,4,64,128]{4,3,2,1,0:T(8,128)(2,1)S(1)}, u32[]{:S(2)}, u32[]{:S(2)}) %collective-permute-start.74) | collective-permute-done | bytes 131104 | tf_op jit(solution)/shard_map/ppermute | solution.py:8
  673.7 15.9 %all_to_all.5 = bf16[4,1,1,16,64,128]{5,4,3,2,1,0:T(8,128)(2,1)S(1)} all-to-all(bf16[4,1,1,16,64,128]{5,4,3,2,1,0:T(8,128)(2,1)S(1)} %pad_maximum_fusion), channel_id=1, replica_groups=mesh['segment'=4,'blk'=64] {'segment'}, dimensions={0} | all-to-all | bytes 2097152 | tf_op jit(solution)/shard_map/all_to_all | solution.py:87
  (247 shorter events, 212.0 us)
Async XLA Ops:
  1.0 28.4 %collective-permute-start = (bf16[16,64,128]{2,1,0:T(8,128)(2,1)S(1)}, bf16[16,64,128]{2,1,0:T(8,128)(2,1)S(1)}, u32[]{:S(2)}, u32[]{:S(2)}) collective-permute-start(bf16[16,64,128]{2,1,0:T(8,128)(2,1)S(1)} %select_bitcast_fusion), channel_id=1, source_target_pairs={{0,1},{1,0},{2,3},{3,2},{4,5},{5,4},{6,7},{7,6},{8,9},{9,8},{10,11... | collective-permute-start | bytes 786440 | tf_op jit(solution)/shard_map/ppermute | solution.py:8
  38.5 6.0 collective-permute-start.1
  44.6 8.7 %collective-permute-start.2 = (bf16[4,1,2,64,128]{4,3,2,1,0:T(8,128)(2,1)S(1)}, bf16[4,1,2,64,128]{4,3,2,1,0:T(8,128)(2,1)S(1)}, u32[]{:S(2)}, u32[]{:S(2)}) collective-permute-start(bf16[4,1,2,64,128]{4,3,2,1,0:T(8,128)(2,1)S(1)} %constant_dynamic-slice_fusion.54), channel_id=1, source_target_pairs={{0,4},{1,5},{2,6},{3,7},{4,0},{5,1},{6,2},{7,3},{8,12},{9,13},{10,... | collective-permute-start | bytes 393224 | tf_op jit(solution)/shard_map/ppermute | solution.py:8
  53.4 12.4 %collective-permute-start.3 = (bf16[2,1,4,64,128]{4,3,2,1,0:T(8,128)(2,1)S(1)}, bf16[2,1,4,64,128]{4,3,2,1,0:T(8,128)(2,1)S(1)}, u32[]{:S(2)}, u32[]{:S(2)}) collective-permute-start(bf16[2,1,4,64,128]{4,3,2,1,0:T(8,128)(2,1)S(1)} %constant_dynamic-slice_fusion.53), channel_id=1, source_target_pairs={{0,8},{1,9},{2,10},{3,11},{4,12},{5,13},{6,14},{7,15},{8,0},{9,1},... | collective-permute-start | bytes 393224 | tf_op jit(solution)/shard_map/ppermute | solution.py:8
  65.8 14.4 %collective-permute-start.4 = (bf16[1,1,8,64,128]{4,3,2,1,0:T(8,128)(2,1)S(1)}, bf16[1,1,8,64,128]{4,3,2,1,0:T(8,128)(2,1)S(1)}, u32[]{:S(2)}, u32[]{:S(2)}) collective-permute-start(bf16[1,1,8,64,128]{4,3,2,1,0:T(8,128)(2,1)S(1)} %constant_dynamic-slice_fusion.52), channel_id=1, source_target_pairs={{0,16},{1,17},{2,18},{3,19},{4,20},{5,21},{6,22},{7,23},{8,24},{9,... | collective-permute-start | bytes 393224 | tf_op jit(solution)/shard_map/ppermute | solution.py:8
  80.2 11.9 %collective-permute-start.5 = (bf16[16,64,128]{2,1,0:T(8,128)(2,1)S(1)}, bf16[16,64,128]{2,1,0:T(8,128)(2,1)S(1)}, u32[]{:S(2)}, u32[]{:S(2)}) collective-permute-start(bf16[16,64,128]{2,1,0:T(8,128)(2,1)S(1)} %bitcast.335), channel_id=1, source_target_pairs={{0,32},{1,33},{2,34},{3,35},{4,36},{5,37},{6,38},{7,39},{8,40},{9,... | collective-permute-start | bytes 786440 | tf_op jit(solution)/shard_map/ppermute | solution.py:8
  101.4 5.1 collective-permute-start.6
  106.5 7.0 %collective-permute-start.7 = (bf16[4,1,2,64,128]{4,3,2,1,0:T(8,128)(2,1)S(1)}, bf16[4,1,2,64,128]{4,3,2,1,0:T(8,128)(2,1)S(1)}, u32[]{:S(2)}, u32[]{:S(2)}) collective-permute-start(bf16[4,1,2,64,128]{4,3,2,1,0:T(8,128)(2,1)S(1)} %constant_dynamic-slice_fusion.50), channel_id=1, source_target_pairs={{0,4},{1,5},{2,6},{3,7},{4,0},{5,1},{6,2},{7,3},{8,12},{9,13},{10,... | collective-permute-start | bytes 393224 | tf_op jit(solution)/shard_map/ppermute | solution.py:8
  113.5 9.8 %collective-permute-start.8 = (bf16[2,1,4,64,128]{4,3,2,1,0:T(8,128)(2,1)S(1)}, bf16[2,1,4,64,128]{4,3,2,1,0:T(8,128)(2,1)S(1)}, u32[]{:S(2)}, u32[]{:S(2)}) collective-permute-start(bf16[2,1,4,64,128]{4,3,2,1,0:T(8,128)(2,1)S(1)} %constant_dynamic-slice_fusion.49), channel_id=1, source_target_pairs={{0,8},{1,9},{2,10},{3,11},{4,12},{5,13},{6,14},{7,15},{8,0},{9,1},... | collective-permute-start | bytes 393224 | tf_op jit(solution)/shard_map/ppermute | solution.py:8
  123.4 5.1 collective-permute-start.9
  128.5 7.4 %collective-permute-start.10 = (bf16[16,64,128]{2,1,0:T(8,128)(2,1)S(1)}, bf16[16,64,128]{2,1,0:T(8,128)(2,1)S(1)}, u32[]{:S(2)}, u32[]{:S(2)}) collective-permute-start(bf16[16,64,128]{2,1,0:T(8,128)(2,1)S(1)} %bitcast.355), channel_id=1, source_target_pairs={{0,64},{64,128},{128,192},{1,65},{65,129},{129,193},{2,66},{66,130... | collective-permute-start | bytes 786440 | tf_op jit(solution)/shard_map/ppermute | solution.py:14
  152.6 7.5 %collective-permute-start.13 = (bf16[4,1,2,64,128]{4,3,2,1,0:T(8,128)(2,1)S(1)}, bf16[4,1,2,64,128]{4,3,2,1,0:T(8,128)(2,1)S(1)}, u32[]{:S(2)}, u32[]{:S(2)}) collective-permute-start(bf16[4,1,2,64,128]{4,3,2,1,0:T(8,128)(2,1)S(1)} %constant_dynamic-slice_fusion.46), channel_id=1, source_target_pairs={{0,4},{1,5},{2,6},{3,7},{4,0},{5,1},{6,2},{7,3},{8,12},{9,13},{10,... | collective-permute-start | bytes 393224 | tf_op jit(solution)/shard_map/ppermute | solution.py:8
  160.1 11.3 %collective-permute-start.14 = (bf16[2,1,4,64,128]{4,3,2,1,0:T(8,128)(2,1)S(1)}, bf16[2,1,4,64,128]{4,3,2,1,0:T(8,128)(2,1)S(1)}, u32[]{:S(2)}, u32[]{:S(2)}) collective-permute-start(bf16[2,1,4,64,128]{4,3,2,1,0:T(8,128)(2,1)S(1)} %constant_dynamic-slice_fusion.45), channel_id=1, source_target_pairs={{0,8},{1,9},{2,10},{3,11},{4,12},{5,13},{6,14},{7,15},{8,0},{9,1},... | collective-permute-start | bytes 393224 | tf_op jit(solution)/shard_map/ppermute | solution.py:8
  171.4 5.2 collective-permute-start.15
  176.6 9.0 %collective-permute-start.16 = (bf16[16,64,128]{2,1,0:T(8,128)(2,1)S(1)}, bf16[16,64,128]{2,1,0:T(8,128)(2,1)S(1)}, u32[]{:S(2)}, u32[]{:S(2)}) collective-permute-start(bf16[16,64,128]{2,1,0:T(8,128)(2,1)S(1)} %bitcast.364), channel_id=1, source_target_pairs={{0,32},{1,33},{2,34},{3,35},{4,36},{5,37},{6,38},{7,39},{8,40},{9,... | collective-permute-start | bytes 786440 | tf_op jit(solution)/shard_map/ppermute | solution.py:8
  197.0 7.1 %collective-permute-start.18 = (bf16[4,1,2,64,128]{4,3,2,1,0:T(8,128)(2,1)S(1)}, bf16[4,1,2,64,128]{4,3,2,1,0:T(8,128)(2,1)S(1)}, u32[]{:S(2)}, u32[]{:S(2)}) collective-permute-start(bf16[4,1,2,64,128]{4,3,2,1,0:T(8,128)(2,1)S(1)} %constant_dynamic-slice_fusion.42), channel_id=1, source_target_pairs={{0,4},{1,5},{2,6},{3,7},{4,0},{5,1},{6,2},{7,3},{8,12},{9,13},{10,... | collective-permute-start | bytes 393224 | tf_op jit(solution)/shard_map/ppermute | solution.py:8
  204.1 10.4 %collective-permute-start.19 = (bf16[2,1,4,64,128]{4,3,2,1,0:T(8,128)(2,1)S(1)}, bf16[2,1,4,64,128]{4,3,2,1,0:T(8,128)(2,1)S(1)}, u32[]{:S(2)}, u32[]{:S(2)}) collective-permute-start(bf16[2,1,4,64,128]{4,3,2,1,0:T(8,128)(2,1)S(1)} %constant_dynamic-slice_fusion.41), channel_id=1, source_target_pairs={{0,8},{1,9},{2,10},{3,11},{4,12},{5,13},{6,14},{7,15},{8,0},{9,1},... | collective-permute-start | bytes 393224 | tf_op jit(solution)/shard_map/ppermute | solution.py:8
  214.5 5.1 collective-permute-start.20
  219.6 8.3 %collective-permute-start.21 = (bf16[16,64,128]{2,1,0:T(8,128)(2,1)S(1)}, bf16[16,64,128]{2,1,0:T(8,128)(2,1)S(1)}, u32[]{:S(2)}, u32[]{:S(2)}) collective-permute-start(bf16[16,64,128]{2,1,0:T(8,128)(2,1)S(1)} %bitcast.374), channel_id=1, source_target_pairs={{0,64},{64,128},{128,192},{1,65},{65,129},{129,193},{2,66},{66,130... | collective-permute-start | bytes 786440 | tf_op jit(solution)/shard_map/ppermute | solution.py:14
  235.8 5.6 collective-permute-start.23
  241.5 8.5 %collective-permute-start.24 = (bf16[4,1,2,64,128]{4,3,2,1,0:T(8,128)(2,1)S(1)}, bf16[4,1,2,64,128]{4,3,2,1,0:T(8,128)(2,1)S(1)}, u32[]{:S(2)}, u32[]{:S(2)}) collective-permute-start(bf16[4,1,2,64,128]{4,3,2,1,0:T(8,128)(2,1)S(1)} %constant_dynamic-slice_fusion.38), channel_id=1, source_target_pairs={{0,4},{1,5},{2,6},{3,7},{4,0},{5,1},{6,2},{7,3},{8,12},{9,13},{10,... | collective-permute-start | bytes 393224 | tf_op jit(solution)/shard_map/ppermute | solution.py:8
  250.0 11.8 %collective-permute-start.25 = (bf16[2,1,4,64,128]{4,3,2,1,0:T(8,128)(2,1)S(1)}, bf16[2,1,4,64,128]{4,3,2,1,0:T(8,128)(2,1)S(1)}, u32[]{:S(2)}, u32[]{:S(2)}) collective-permute-start(bf16[2,1,4,64,128]{4,3,2,1,0:T(8,128)(2,1)S(1)} %constant_dynamic-slice_fusion.37), channel_id=1, source_target_pairs={{0,8},{1,9},{2,10},{3,11},{4,12},{5,13},{6,14},{7,15},{8,0},{9,1},... | collective-permute-start | bytes 393224 | tf_op jit(solution)/shard_map/ppermute | solution.py:8
  261.9 5.5 collective-permute-start.26
  267.4 9.2 %collective-permute-start.27 = (bf16[16,64,128]{2,1,0:T(8,128)(2,1)S(1)}, bf16[16,64,128]{2,1,0:T(8,128)(2,1)S(1)}, u32[]{:S(2)}, u32[]{:S(2)}) collective-permute-start(bf16[16,64,128]{2,1,0:T(8,128)(2,1)S(1)} %bitcast.383), channel_id=1, source_target_pairs={{0,32},{1,33},{2,34},{3,35},{4,36},{5,37},{6,38},{7,39},{8,40},{9,... | collective-permute-start | bytes 786440 | tf_op jit(solution)/shard_map/ppermute | solution.py:8
  282.8 5.1 collective-permute-start.28
  287.9 6.9 collective-permute-start.29
  294.8 10.3 %collective-permute-start.30 = (bf16[2,1,4,64,128]{4,3,2,1,0:T(8,128)(2,1)S(1)}, bf16[2,1,4,64,128]{4,3,2,1,0:T(8,128)(2,1)S(1)}, u32[]{:S(2)}, u32[]{:S(2)}) collective-permute-start(bf16[2,1,4,64,128]{4,3,2,1,0:T(8,128)(2,1)S(1)} %constant_dynamic-slice_fusion.33), channel_id=1, source_target_pairs={{0,8},{1,9},{2,10},{3,11},{4,12},{5,13},{6,14},{7,15},{8,0},{9,1},... | collective-permute-start | bytes 393224 | tf_op jit(solution)/shard_map/ppermute | solution.py:8
  310.2 8.3 %collective-permute-start.32 = (bf16[16,64,128]{2,1,0:T(8,128)(2,1)S(1)}, bf16[16,64,128]{2,1,0:T(8,128)(2,1)S(1)}, u32[]{:S(2)}, u32[]{:S(2)}) collective-permute-start(bf16[16,64,128]{2,1,0:T(8,128)(2,1)S(1)} %bitcast.393), channel_id=1, source_target_pairs={{0,64},{64,128},{128,192},{1,65},{65,129},{129,193},{2,66},{66,130... | collective-permute-start | bytes 786440 | tf_op jit(solution)/shard_map/ppermute | solution.py:14
  326.7 5.6 collective-permute-start.34
  332.4 8.5 %collective-permute-start.35 = (bf16[4,1,2,64,128]{4,3,2,1,0:T(8,128)(2,1)S(1)}, bf16[4,1,2,64,128]{4,3,2,1,0:T(8,128)(2,1)S(1)}, u32[]{:S(2)}, u32[]{:S(2)}) collective-permute-start(bf16[4,1,2,64,128]{4,3,2,1,0:T(8,128)(2,1)S(1)} %constant_dynamic-slice_fusion.30), channel_id=1, source_target_pairs={{0,4},{1,5},{2,6},{3,7},{4,0},{5,1},{6,2},{7,3},{8,12},{9,13},{10,... | collective-permute-start | bytes 393224 | tf_op jit(solution)/shard_map/ppermute | solution.py:8
  340.9 11.8 %collective-permute-start.36 = (bf16[2,1,4,64,128]{4,3,2,1,0:T(8,128)(2,1)S(1)}, bf16[2,1,4,64,128]{4,3,2,1,0:T(8,128)(2,1)S(1)}, u32[]{:S(2)}, u32[]{:S(2)}) collective-permute-start(bf16[2,1,4,64,128]{4,3,2,1,0:T(8,128)(2,1)S(1)} %constant_dynamic-slice_fusion.29), channel_id=1, source_target_pairs={{0,8},{1,9},{2,10},{3,11},{4,12},{5,13},{6,14},{7,15},{8,0},{9,1},... | collective-permute-start | bytes 393224 | tf_op jit(solution)/shard_map/ppermute | solution.py:8
  352.8 5.5 collective-permute-start.37
  358.3 9.1 %collective-permute-start.38 = (bf16[16,64,128]{2,1,0:T(8,128)(2,1)S(1)}, bf16[16,64,128]{2,1,0:T(8,128)(2,1)S(1)}, u32[]{:S(2)}, u32[]{:S(2)}) collective-permute-start(bf16[16,64,128]{2,1,0:T(8,128)(2,1)S(1)} %bitcast.402), channel_id=1, source_target_pairs={{0,32},{1,33},{2,34},{3,35},{4,36},{5,37},{6,38},{7,39},{8,40},{9,... | collective-permute-start | bytes 786440 | tf_op jit(solution)/shard_map/ppermute | solution.py:8
  373.7 5.1 collective-permute-start.39
  378.8 6.9 collective-permute-start.40
  385.7 10.3 %collective-permute-start.41 = (bf16[2,1,4,64,128]{4,3,2,1,0:T(8,128)(2,1)S(1)}, bf16[2,1,4,64,128]{4,3,2,1,0:T(8,128)(2,1)S(1)}, u32[]{:S(2)}, u32[]{:S(2)}) collective-permute-start(bf16[2,1,4,64,128]{4,3,2,1,0:T(8,128)(2,1)S(1)} %constant_dynamic-slice_fusion.25), channel_id=1, source_target_pairs={{0,8},{1,9},{2,10},{3,11},{4,12},{5,13},{6,14},{7,15},{8,0},{9,1},... | collective-permute-start | bytes 393224 | tf_op jit(solution)/shard_map/ppermute | solution.py:8
  401.1 8.3 %collective-permute-start.43 = (bf16[16,64,128]{2,1,0:T(8,128)(2,1)S(1)}, bf16[16,64,128]{2,1,0:T(8,128)(2,1)S(1)}, u32[]{:S(2)}, u32[]{:S(2)}) collective-permute-start(bf16[16,64,128]{2,1,0:T(8,128)(2,1)S(1)} %bitcast.304), channel_id=1, source_target_pairs={{0,64},{64,128},{128,192},{1,65},{65,129},{129,193},{2,66},{66,130... | collective-permute-start | bytes 786440 | tf_op jit(solution)/shard_map/ppermute | solution.py:14
  417.4 5.6 collective-permute-start.45
  423.1 8.5 %collective-permute-start.46 = (bf16[4,1,2,64,128]{4,3,2,1,0:T(8,128)(2,1)S(1)}, bf16[4,1,2,64,128]{4,3,2,1,0:T(8,128)(2,1)S(1)}, u32[]{:S(2)}, u32[]{:S(2)}) collective-permute-start(bf16[4,1,2,64,128]{4,3,2,1,0:T(8,128)(2,1)S(1)} %constant_dynamic-slice_fusion.22), channel_id=1, source_target_pairs={{0,4},{1,5},{2,6},{3,7},{4,0},{5,1},{6,2},{7,3},{8,12},{9,13},{10,... | collective-permute-start | bytes 393224 | tf_op jit(solution)/shard_map/ppermute | solution.py:8
  431.6 11.8 %collective-permute-start.47 = (bf16[2,1,4,64,128]{4,3,2,1,0:T(8,128)(2,1)S(1)}, bf16[2,1,4,64,128]{4,3,2,1,0:T(8,128)(2,1)S(1)}, u32[]{:S(2)}, u32[]{:S(2)}) collective-permute-start(bf16[2,1,4,64,128]{4,3,2,1,0:T(8,128)(2,1)S(1)} %constant_dynamic-slice_fusion.21), channel_id=1, source_target_pairs={{0,8},{1,9},{2,10},{3,11},{4,12},{5,13},{6,14},{7,15},{8,0},{9,1},... | collective-permute-start | bytes 393224 | tf_op jit(solution)/shard_map/ppermute | solution.py:8
  443.5 5.5 collective-permute-start.48
  449.0 9.4 %collective-permute-start.49 = (bf16[16,64,128]{2,1,0:T(8,128)(2,1)S(1)}, bf16[16,64,128]{2,1,0:T(8,128)(2,1)S(1)}, u32[]{:S(2)}, u32[]{:S(2)}) collective-permute-start(bf16[16,64,128]{2,1,0:T(8,128)(2,1)S(1)} %bitcast.412), channel_id=1, source_target_pairs={{0,32},{1,33},{2,34},{3,35},{4,36},{5,37},{6,38},{7,39},{8,40},{9,... | collective-permute-start | bytes 786440 | tf_op jit(solution)/shard_map/ppermute | solution.py:8
  469.7 6.9 collective-permute-start.51
  476.6 10.3 %collective-permute-start.52 = (bf16[2,1,4,64,128]{4,3,2,1,0:T(8,128)(2,1)S(1)}, bf16[2,1,4,64,128]{4,3,2,1,0:T(8,128)(2,1)S(1)}, u32[]{:S(2)}, u32[]{:S(2)}) collective-permute-start(bf16[2,1,4,64,128]{4,3,2,1,0:T(8,128)(2,1)S(1)} %constant_dynamic-slice_fusion.17), channel_id=1, source_target_pairs={{0,8},{1,9},{2,10},{3,11},{4,12},{5,13},{6,14},{7,15},{8,0},{9,1},... | collective-permute-start | bytes 393224 | tf_op jit(solution)/shard_map/ppermute | solution.py:8
  487.0 5.1 collective-permute-start.53
  492.0 8.3 %collective-permute-start.54 = (bf16[16,64,128]{2,1,0:T(8,128)(2,1)S(1)}, bf16[16,64,128]{2,1,0:T(8,128)(2,1)S(1)}, u32[]{:S(2)}, u32[]{:S(2)}) collective-permute-start(bf16[16,64,128]{2,1,0:T(8,128)(2,1)S(1)} %bitcast.314), channel_id=1, source_target_pairs={{0,64},{64,128},{128,192},{1,65},{65,129},{129,193},{2,66},{66,130... | collective-permute-start | bytes 786440 | tf_op jit(solution)/shard_map/ppermute | solution.py:14
  508.3 5.6 collective-permute-start.56
  514.0 8.5 %collective-permute-start.57 = (bf16[4,1,2,64,128]{4,3,2,1,0:T(8,128)(2,1)S(1)}, bf16[4,1,2,64,128]{4,3,2,1,0:T(8,128)(2,1)S(1)}, u32[]{:S(2)}, u32[]{:S(2)}) collective-permute-start(bf16[4,1,2,64,128]{4,3,2,1,0:T(8,128)(2,1)S(1)} %constant_dynamic-slice_fusion.14), channel_id=1, source_target_pairs={{0,4},{1,5},{2,6},{3,7},{4,0},{5,1},{6,2},{7,3},{8,12},{9,13},{10,... | collective-permute-start | bytes 393224 | tf_op jit(solution)/shard_map/ppermute | solution.py:8
  522.5 11.8 %collective-permute-start.58 = (bf16[2,1,4,64,128]{4,3,2,1,0:T(8,128)(2,1)S(1)}, bf16[2,1,4,64,128]{4,3,2,1,0:T(8,128)(2,1)S(1)}, u32[]{:S(2)}, u32[]{:S(2)}) collective-permute-start(bf16[2,1,4,64,128]{4,3,2,1,0:T(8,128)(2,1)S(1)} %constant_dynamic-slice_fusion.13), channel_id=1, source_target_pairs={{0,8},{1,9},{2,10},{3,11},{4,12},{5,13},{6,14},{7,15},{8,0},{9,1},... | collective-permute-start | bytes 393224 | tf_op jit(solution)/shard_map/ppermute | solution.py:8
  534.4 5.5 collective-permute-start.59
  539.9 9.2 %collective-permute-start.60 = (bf16[16,64,128]{2,1,0:T(8,128)(2,1)S(1)}, bf16[16,64,128]{2,1,0:T(8,128)(2,1)S(1)}, u32[]{:S(2)}, u32[]{:S(2)}) collective-permute-start(bf16[16,64,128]{2,1,0:T(8,128)(2,1)S(1)} %bitcast.422), channel_id=1, source_target_pairs={{0,32},{1,33},{2,34},{3,35},{4,36},{5,37},{6,38},{7,39},{8,40},{9,... | collective-permute-start | bytes 786440 | tf_op jit(solution)/shard_map/ppermute | solution.py:8
  555.2 5.1 collective-permute-start.61
  560.3 6.9 collective-permute-start.62
  567.3 10.3 %collective-permute-start.63 = (bf16[2,1,4,64,128]{4,3,2,1,0:T(8,128)(2,1)S(1)}, bf16[2,1,4,64,128]{4,3,2,1,0:T(8,128)(2,1)S(1)}, u32[]{:S(2)}, u32[]{:S(2)}) collective-permute-start(bf16[2,1,4,64,128]{4,3,2,1,0:T(8,128)(2,1)S(1)} %constant_dynamic-slice_fusion.9), channel_id=1, source_target_pairs={{0,8},{1,9},{2,10},{3,11},{4,12},{5,13},{6,14},{7,15},{8,0},{9,1},... | collective-permute-start | bytes 393224 | tf_op jit(solution)/shard_map/ppermute | solution.py:8
  577.6 5.1 collective-permute-start.64
  582.7 8.3 %collective-permute-start.65 = (bf16[16,64,128]{2,1,0:T(8,128)(2,1)S(1)}, bf16[16,64,128]{2,1,0:T(8,128)(2,1)S(1)}, u32[]{:S(2)}, u32[]{:S(2)}) collective-permute-start(bf16[16,64,128]{2,1,0:T(8,128)(2,1)S(1)} %bitcast.324), channel_id=1, source_target_pairs={{0,64},{64,128},{128,192},{1,65},{65,129},{129,193},{2,66},{66,130... | collective-permute-start | bytes 786440 | tf_op jit(solution)/shard_map/ppermute | solution.py:14
  599.2 5.6 collective-permute-start.67
  604.9 8.5 %collective-permute-start.68 = (bf16[4,1,2,64,128]{4,3,2,1,0:T(8,128)(2,1)S(1)}, bf16[4,1,2,64,128]{4,3,2,1,0:T(8,128)(2,1)S(1)}, u32[]{:S(2)}, u32[]{:S(2)}) collective-permute-start(bf16[4,1,2,64,128]{4,3,2,1,0:T(8,128)(2,1)S(1)} %constant_dynamic-slice_fusion.6), channel_id=1, source_target_pairs={{0,4},{1,5},{2,6},{3,7},{4,0},{5,1},{6,2},{7,3},{8,12},{9,13},{10,... | collective-permute-start | bytes 393224 | tf_op jit(solution)/shard_map/ppermute | solution.py:8
  613.4 11.8 %collective-permute-start.69 = (bf16[2,1,4,64,128]{4,3,2,1,0:T(8,128)(2,1)S(1)}, bf16[2,1,4,64,128]{4,3,2,1,0:T(8,128)(2,1)S(1)}, u32[]{:S(2)}, u32[]{:S(2)}) collective-permute-start(bf16[2,1,4,64,128]{4,3,2,1,0:T(8,128)(2,1)S(1)} %constant_dynamic-slice_fusion.5), channel_id=1, source_target_pairs={{0,8},{1,9},{2,10},{3,11},{4,12},{5,13},{6,14},{7,15},{8,0},{9,1},... | collective-permute-start | bytes 393224 | tf_op jit(solution)/shard_map/ppermute | solution.py:8
  625.3 5.5 collective-permute-start.70
  630.8 9.1 %collective-permute-start.71 = (bf16[16,64,128]{2,1,0:T(8,128)(2,1)S(1)}, bf16[16,64,128]{2,1,0:T(8,128)(2,1)S(1)}, u32[]{:S(2)}, u32[]{:S(2)}) collective-permute-start(bf16[16,64,128]{2,1,0:T(8,128)(2,1)S(1)} %bitcast.345), channel_id=1, source_target_pairs={{0,32},{1,33},{2,34},{3,35},{4,36},{5,37},{6,38},{7,39},{8,40},{9,... | collective-permute-start | bytes 786440 | tf_op jit(solution)/shard_map/ppermute | solution.py:8
  651.2 6.9 collective-permute-start.73
  658.2 10.3 %collective-permute-start.74 = (bf16[2,1,4,64,128]{4,3,2,1,0:T(8,128)(2,1)S(1)}, bf16[2,1,4,64,128]{4,3,2,1,0:T(8,128)(2,1)S(1)}, u32[]{:S(2)}, u32[]{:S(2)}) collective-permute-start(bf16[2,1,4,64,128]{4,3,2,1,0:T(8,128)(2,1)S(1)} %constant_dynamic-slice_fusion.1), channel_id=1, source_target_pairs={{0,8},{1,9},{2,10},{3,11},{4,12},{5,13},{6,14},{7,15},{8,0},{9,1},... | collective-permute-start | bytes 393224 | tf_op jit(solution)/shard_map/ppermute | solution.py:8
  668.5 5.1 collective-permute-start.75
  (19 other events, 306.4 us)
